TPU v7x, 256 devices: a whole 4x4x8 slice. The times are simulated.
256 devices in a mesh: tm: 256 (over x, z, y, core).
Axes of the slice: x: 4, y: 4, z: 8, core: 2. Of those that a mesh axis runs over, the one named last changes fastest.
Arguments:
- measurements: float32 [256, 128], P('tm'), may hold values from -6 to 6
- noise_levels: float32 [256, 128], P('tm'), may hold values from 0.05 to 2
- transition: float32 [256, 256], replicated, may hold values from -0.5 to 1.5
- sensing: float32 [128, 256], replicated, may hold values from -0.75 to 0.75
- process_noise: float32 [256, 256], replicated, may hold values from -0.2 to 0.6, as said below
- prior_mean: float32 [256], replicated, may hold values from -5 to 5
- prior_covariance: float32 [256, 256], replicated, may hold values from -0.6 to 2.5, as said below
Outputs:
- smoothed_means: float32 [256, 256], P('tm')
- smoothed_covariances: float32 [256, 256, 256], P('tm')
Inputs may be any that keep to these rules, and one draw needn't show every extreme that they name: `process_noise`: symmetric positive definite. `prior_covariance`: symmetric positive definite.
All inputs are finite; a program needn't handle non-finite values.
Results may differ from a plain program's by a relative error of at most 0.0003.
Values sent between devices are 32-bit elements; how exact they have to be, the bound alone decides.
A program may use at most 128 MiB of HBM per device.

v0:
```python
import functools

import jax
import jax.numpy as jnp
from jax import lax
from jax.experimental import pallas as pl
from jax.experimental.pallas import tpu as pltpu
from jax.sharding import PartitionSpec as P

F32 = jnp.float32
BF16 = jnp.bfloat16
NN = (((1,), (0,)), ((), ()))
NT = (((1,), (1,)), ((), ()))


def exact(left, right, dims=NN):
    return lax.dot_general(
        left, right, dims, precision=lax.Precision.HIGHEST, preferred_element_type=F32
    )


def rough(left, right, dims=NN):
    return lax.dot_general(
        left.astype(BF16), right.astype(BF16), dims, preferred_element_type=F32
    )


def unit(size):
    rows = lax.broadcasted_iota(jnp.int32, (size, size), 0)
    columns = lax.broadcasted_iota(jnp.int32, (size, size), 1)
    return (rows == columns).astype(F32)


def medium(left, right, dims=NN):
    left_high, right_high = left.astype(BF16), right.astype(BF16)
    left_low = (left - left_high.astype(F32)).astype(BF16)
    right_low = (right - right_high.astype(F32)).astype(BF16)

    def times(a, b):
        return lax.dot_general(a, b, dims, preferred_element_type=F32)

    return times(left_high, right_high) + (
        times(left_high, right_low) + times(left_low, right_high)
    )


def inverse(product, bound, pair):
    size = product.shape[0]
    eye = unit(size)
    whole = eye + product
    small = bound < 128.0

    def gain_of(low):
        return 4.0 / ((1.0 + low) * (1.0 + low))

    def more(state):
        return jnp.logical_not(state[1])

    @pl.when(small)
    def _():
        low = 1.0 / bound
        scaled = whole * low
        step = gain_of(low) * ((1.0 + low) * eye - scaled)
        pair[:size, :] = step * low
        pair[size : 2 * size, :] = rough(scaled, step)

        def turn(state):
            low, _ = state
            ends = low >= 0.95
            low = jnp.where(ends, 1.0, low)
            step = gain_of(low) * ((1.0 + low) * eye - pair[size : 2 * size, :])
            pair[: 2 * size, :] = rough(pair[: 2 * size, :], step)
            return low * gain_of(low), ends

        lax.while_loop(more, turn, (low * gain_of(low), jnp.bool_(False)))

    @pl.when(jnp.logical_not(small))
    def _():
        low = 1.0 / bound
        pair[:size, :] = eye * low
        pair[size : 2 * size, :] = whole * low

        def turn(state):
            low, _ = state
            ends = low >= 0.999
            low = jnp.where(ends, 1.0, low)
            pair[2 * size :, :] = gain_of(low) * (
                (1.0 + low) * eye - pair[size : 2 * size, :]
            )

            def block(i, carry):
                at = pl.ds(pl.multiple_of(i * 32, 32), 32)
                pair[at, :] = exact(pair[at, :], pair[2 * size :, :])
                return carry

            lax.fori_loop(0, 2 * size // 32, block, 0)
            return low * gain_of(low), ends

        lax.while_loop(more, turn, (low, jnp.bool_(False)))

    def correct(i, carry):
        guess = pair[:size, :]
        pair[:size, :] = guess + rough(guess, eye - medium(whole, guess))
        return carry

    lax.fori_loop(0, 2, correct, 0)
    return pair[:size, :]


def spectral_bound(product, mirrored):
    return 1.0 + 1.02 * jnp.sqrt(jnp.maximum(jnp.sum(product * mirrored), 0.0))


def pack(out, value, vector):
    ns = value.shape[0]
    n = ns // 2
    rows = lax.broadcasted_iota(jnp.int32, (n, n), 0)
    columns = lax.broadcasted_iota(jnp.int32, (n, n), 1)
    low, high = value[:n, :n], value[n:, n:]
    out[:n, :n] = value[n:, :n]
    out[:n, n:] = jnp.where(rows >= columns, low, high)
    out[n : n + 8, :] = jnp.zeros((8, ns), F32)
    out[n : n + 1, :] = vector[:1, :]
    out[n + 1 : n + 2, :n] = jnp.sum(
        jnp.where(rows == columns, high, 0.0), axis=0, keepdims=True
    )


def unpack(ref):
    ns = ref.shape[1]
    n = ns // 2
    rows = lax.broadcasted_iota(jnp.int32, (n, n), 0)
    columns = lax.broadcasted_iota(jnp.int32, (n, n), 1)
    corner = ref[:n, :n]
    mixed = ref[:n, n:]
    turned = mixed.T
    diagonal = jnp.broadcast_to(ref[n + 1 : n + 2, :n], (n, n))
    low = jnp.where(rows >= columns, mixed, turned)
    high = jnp.where(rows < columns, mixed, jnp.where(rows == columns, diagonal, turned))
    value = jnp.concatenate(
        [
            jnp.concatenate([low, corner.T], axis=1),
            jnp.concatenate([corner, high], axis=1),
        ],
        axis=0,
    )
    return value, spread_rows(ref, n)


def spread_rows(ref, at):
    return jnp.broadcast_to(ref[at : at + 1, :], (8, ref.shape[1]))


def fill(ref, value, vector):
    ns = value.shape[1]
    ref[:ns, :] = value
    ref[ns:, :] = vector


def resolve(x_ref, y_ref, out, pair):
    ns = x_ref.shape[1]
    value = y_ref[:ns, :]
    both = medium(x_ref[...], value)
    product = both[:ns, :]
    bound = spectral_bound(product, rough(value, x_ref[:ns, :]))
    out[:ns, :] = inverse(product, bound, pair)
    out[ns:, :] = y_ref[ns:, :] - both[ns:, :]


def later_spread(through, x_ref, move, s_ref, out):
    ns = x_ref.shape[1]
    carried = medium(through[...], x_ref[:ns, :])
    offset = exact(x_ref[ns:, :] + carried[ns:, :], through[:ns, :], NT)
    fill(out, medium(carried[:ns, :], move, NT) + s_ref[:ns, :], offset + s_ref[ns:, :])


def start_kernel(
    place_ref, mine_ref, other_ref, f_hbm, h_hbm, q_hbm, m_ref, p_hbm,
    leaves, x_out, y_out,
    f_ref, h_ref, noise, p_ref, center, plain, sensed_plain, inner_plain, half_pair, sems,
):
    chip, core = lax.div(place_ref[0], 2), lax.rem(place_ref[0], 2)
    lead = core == 0
    no, ns = h_ref.shape
    tall = ns + 8
    size = 2 * tall + ns
    copies = [
        pltpu.make_async_copy(source, target, sems.at[i])
        for i, (source, target) in enumerate(((h_hbm, h_ref), (f_hbm, f_ref), (q_hbm, noise)))
    ]
    for copy in copies:
        copy.start()
    center[...] = jnp.zeros_like(center)
    eye = unit(no)
    copies[0].wait()
    copies[1].wait()
    sensed_plain[...] = exact(h_ref[...], f_ref[...])
    copies[2].wait()

    def leaf(i, carry):
        first = jnp.logical_and(i == 1, chip == 0)
        own = (i == 1) == lead
        at = pl.multiple_of(i * size, 8)

        @pl.when(first)
        def _():
            copy = pltpu.make_async_copy(p_hbm, p_ref, sems.at[3])
            copy.start()
            copy.wait()
            noise[...] += exact(exact(f_ref[...], p_ref[...]), f_ref[...], NT)
            center[...] = exact(jnp.broadcast_to(m_ref[...], center.shape), f_ref[...], NT)

        @pl.when(jnp.logical_or(i == 0, first))
        def _():
            plain[...] = exact(h_ref[...], noise[...])
            inner_plain[...] = exact(plain[...], h_ref[...], NT)

        weight = lax.rsqrt(jnp.where(own, mine_ref[1:2, :], other_ref[1:2, :]))
        y = jnp.where(own, mine_ref[:1, :], other_ref[:1, :]) * weight
        y = jnp.broadcast_to(y, (8, no))
        weights = jnp.sum(eye * weight, axis=1, keepdims=True)
        gain = plain[...] * weights
        sensed = sensed_plain[...] * weights
        inner = inner_plain[...] * weights * weight
        active = jnp.where(first, 0.0, 1.0)
        mixed = inverse(inner, spectral_bound(inner, inner), half_pair)
        gained = exact(mixed, gain)
        joined = exact(mixed, sensed)
        gain_t = gain.T
        error = y - exact(center[...], h_ref[...], NT) * weight
        leaves[pl.ds(at, ns), :] = active * (f_ref[...] - exact(gain_t, joined))
        leaves[pl.ds(at + ns, ns), :] = noise[...] - exact(gain_t, gained)
        leaves[pl.ds(at + 2 * ns, 8), :] = center[...] + exact(error, gained)
        leaves[pl.ds(at + ns + tall, ns), :] = active * medium(sensed.T, joined)
        leaves[pl.ds(at + 2 * ns + tall, 8), :] = active * exact(y, joined)
        return carry

    lax.fori_loop(0, 2, leaf, 0)
    x_out[...] = leaves[size + ns : size + ns + tall, :]
    y_out[...] = leaves[ns + tall : size, :]


def pair_kernel(
    place_ref, solved, leaves, s_out, move_out, bind_out, y_out, spread_msg, through
):
    ns = solved.shape[1]
    tall = ns + 8
    size = 2 * tall + ns
    odd, even = leaves.at[:size, :], leaves.at[size:, :]
    lead = lax.rem(place_ref[0], 2) == 0
    x_ref = even.at[ns : ns + tall, :]
    y_ref = odd.at[ns + tall :, :]
    later = odd[:ns, :]
    early = even[:ns, :]
    fill(through, exact(later, solved[:ns, :]), y_ref[ns:, :])
    later_spread(through, x_ref, later, odd.at[ns : ns + tall, :], s_out)
    pack(spread_msg, s_out[:ns, :], s_out[ns:, :])
    move_out[...] = exact(through[:ns, :], early)
    fill(through, y_ref[:ns, :], solved[ns:, :])
    both = medium(medium(through[...], solved[:ns, :]), early)
    bind = medium(early.T, both[:ns, :]) + even[ns + tall : ns + tall + ns, :]
    pull = both[ns:, :] + even[2 * ns + tall :, :]
    pack(bind_out, bind, pull)
    scale = jnp.where(lead, 1.0, 0.0)
    fill(y_out, scale * bind, scale * pull)


def resolve_kernel(x_ref, y_ref, out, pair):
    resolve(x_ref, y_ref, out, pair)


def greet(mine, count, cases):
    barrier = pltpu.get_barrier_semaphore()
    expected = jnp.int32(0)
    for wanted, hop in cases:
        inside = jnp.logical_and(mine + hop >= 0, mine + hop < count)
        inside = jnp.logical_and(inside, wanted)
        expected = expected + inside.astype(jnp.int32)

        @pl.when(inside)
        def _(hop=hop):
            pl.semaphore_signal(
                barrier, inc=1, device_id=(mine + hop,), device_id_type=pl.DeviceIdType.MESH
            )


    def arrive():
        @pl.when(expected > 0)
        def _():
            pl.semaphore_wait(barrier, expected)

    return arrive


def shift_kernel(hop, count, message, s_ref, x_out, land, send_sem, recv_sem):
    mine = lax.axis_index("tm")
    lead = lax.rem(mine, 2) == 0
    side = jnp.logical_not(lead)
    arrive = greet(mine, count, [(lead, hop), (lead, -hop)])
    copy = pltpu.make_async_remote_copy(
        src_ref=message,
        dst_ref=land,
        send_sem=send_sem,
        recv_sem=recv_sem,
        device_id=(lax.rem(mine + hop, count),),
        device_id_type=pl.DeviceIdType.MESH,
    )
    sends = jnp.logical_and(lead, mine + hop < count)
    takes = jnp.logical_and(lead, mine - hop >= 0)
    arrive()
    pl.when(sends)(copy.start)

    @pl.when(side)
    def _():
        x_out[...] = s_ref[...]

    @pl.when(jnp.logical_and(lead, mine - hop < 0))
    def _():
        x_out[...] = jnp.zeros_like(x_out)

    @pl.when(takes)
    def _():
        copy.wait_recv()
        fill(x_out, *unpack(land))

    pl.when(sends)(copy.wait_send)


def exchange_kernel(
    hop, spread_hop, count, last,
    solved, x_ref, y_ref, s_ref, move_ref, bind_ref,
    x_out, y_out, s_out, move_out, bind_out,
    middle, through, spread_msg, bind_msg, move_land, pull_land, spread_land, bind_land,
    send_sems, recv_sems,
):
    ns = x_ref.shape[1]
    mine = lax.axis_index("tm")
    lead = lax.rem(mine, 2) == 0
    side = jnp.logical_not(lead)
    cases = [(lead, 1), (side, -1), (lead, spread_hop), (lead, -spread_hop)]
    if last:
        cases += [(side, hop), (side, -hop)]
    else:
        cases += [(True, hop), (True, -hop)]
    arrive = greet(mine, count, cases)

    def carry(source, land, send, recv, by):
        return pltpu.make_async_remote_copy(
            src_ref=source,
            dst_ref=land,
            send_sem=send_sems.at[send],
            recv_sem=recv_sems.at[recv],
            device_id=(lax.rem(mine + by + count, count),),
            device_id_type=pl.DeviceIdType.MESH,
        )

    def reaches(by):
        return jnp.logical_and(mine + by >= 0, mine + by < count)

    move_side = carry(move_ref, move_land, 0, 0, 1)
    pull_side = carry(bind_ref, pull_land, 1, 1, 1)
    spread_up = carry(spread_msg, spread_land, 2, 2, spread_hop)
    spread_side = carry(spread_msg, spread_land, 3, 2, 1)
    bind_down = carry(bind_msg, bind_land, 4, 3, -hop)
    move_sends = jnp.logical_and(lead, reaches(hop))
    spread_sends = jnp.logical_and(lead, reaches(spread_hop))
    bind_sends = jnp.logical_and(side, reaches(-hop))
    spread_takes = jnp.logical_or(side, reaches(-spread_hop))
    if last:
        move_takes = side
    else:
        move_up = carry(move_ref, move_land, 5, 0, hop)
        pull_up = carry(bind_ref, pull_land, 6, 1, hop)
        move_takes = jnp.logical_or(side, reaches(-hop))

    @pl.when(lead)
    def _():
        fill(through, exact(move_ref[...], solved[:ns, :]), y_ref[ns:, :])

    arrive()
    if not last:

        @pl.when(move_sends)
        def _():
            move_up.start()
            pull_up.start()

    @pl.when(lead)
    def _():
        move_side.start()
        pull_side.start()

    def mix():
        fill(middle, y_ref[:ns, :], solved[ns:, :])
        middle[...] = medium(middle[...], solved[:ns, :])

    if last:
        pl.when(side)(mix)
    else:
        mix()

    @pl.when(lead)
    def _():
        later_spread(through, x_ref, move_ref[...], s_ref, s_out)
        pack(spread_msg, s_out[:ns, :], s_out[ns:, :])

    pl.when(spread_sends)(spread_up.start)
    pl.when(lead)(spread_side.start)

    @pl.when(move_takes)
    def _():
        move_side.wait_recv()

    @pl.when(jnp.logical_not(move_takes))
    def _():
        move_land[...] = jnp.zeros_like(move_land)
        pull_land[...] = jnp.zeros_like(pull_land)

    def rest():
        early = move_land[...]
        both = medium(middle[...], early)
        bind = medium(early.T, both[:ns, :])

        @pl.when(move_takes)
        def _():
            pull_side.wait_recv()

        bind_i, pull_i = unpack(pull_land)
        fill(y_out, bind + bind_i, both[ns:, :] + pull_i)
        pack(bind_msg, y_out[:ns, :], y_out[ns:, :])

    if last:
        pl.when(side)(rest)
    else:
        rest()
    pl.when(bind_sends)(bind_down.start)
    if not last:

        @pl.when(lead)
        def _():
            move_out[...] = exact(through[:ns, :], move_land[...])
            bind_out[...] = bind_msg[...]

    @pl.when(spread_takes)
    def _():
        spread_side.wait_recv()
        fill(x_out, *unpack(spread_land))

    @pl.when(jnp.logical_not(spread_takes))
    def _():
        x_out[...] = jnp.zeros_like(x_out)

    @pl.when(jnp.logical_and(side, reaches(hop)))
    def _():
        bind_down.wait_recv()
        fill(y_out, *unpack(bind_land))

    @pl.when(jnp.logical_and(side, jnp.logical_not(reaches(hop))))
    def _():
        y_out[...] = y_ref[...]

    if not last:

        @pl.when(move_sends)
        def _():
            move_up.wait_send()
            pull_up.wait_send()

    @pl.when(lead)
    def _():
        move_side.wait_send()
        pull_side.wait_send()

    pl.when(spread_sends)(spread_up.wait_send)
    pl.when(lead)(spread_side.wait_send)
    pl.when(bind_sends)(bind_down.wait_send)


def choose_kernel(place_ref, x_ref, y_ref, leaves, left, right):
    ns = x_ref.shape[1]
    tall = ns + 8
    core = lax.rem(place_ref[0], 2)
    odd, even = leaves.at[: 2 * tall + ns, :], leaves.at[2 * tall + ns :, :]

    @pl.when(core == 0)
    def _():
        left[...] = x_ref[...]
        right[...] = even[ns + tall :, :]

    @pl.when(core != 0)
    def _():
        left[...] = odd[ns : ns + tall, :]
        right[...] = y_ref[...]


def finish_kernel(count, solved, x_ref, y_ref, leaves, s_out, y_out, middle, message, land, send_sem, recv_sem):
    ns = x_ref.shape[1]
    tall = ns + 8
    mine = lax.axis_index("tm")
    lead = lax.rem(mine, 2) == 0
    side = jnp.logical_not(lead)
    odd, even = leaves.at[: 2 * tall + ns, :], leaves.at[2 * tall + ns :, :]
    arrive = greet(mine, count, [(lead, 1), (side, -1)])
    copy = pltpu.make_async_remote_copy(
        src_ref=message,
        dst_ref=land,
        send_sem=send_sem,
        recv_sem=recv_sem,
        device_id=(lax.rem(mine - 1 + count, count),),
        device_id_type=pl.DeviceIdType.MESH,
    )

    @pl.when(lead)
    def _():
        move = even[:ns, :]
        fill(middle, exact(move, solved[:ns, :]), even[2 * ns + tall :, :])
        later_spread(middle, x_ref, move, even.at[ns : ns + tall, :], s_out)

    @pl.when(side)
    def _():
        move = odd[:ns, :]
        fill(middle, y_ref[:ns, :], solved[ns:, :])
        both = medium(medium(middle[...], solved[:ns, :]), move)
        bind = medium(move.T, both[:ns, :]) + odd[ns + tall : 2 * ns + tall, :]
        pack(message, bind, both[ns:, :] + odd[2 * ns + tall :, :])
        s_out[...] = x_ref[...]
        y_out[...] = y_ref[...]

    arrive()

    @pl.when(side)
    def _():
        copy.start()
        copy.wait_send()

    @pl.when(lead)
    def _():
        copy.wait_recv()
        fill(y_out, *unpack(land))


def last_kernel(solved, own_ref, later_ref, mean_ref, cov_ref):
    ns = own_ref.shape[1]
    mixed = solved[:ns, :]
    whole = own_ref[:ns, :]
    cov_ref[...] = exact(mixed, whole)
    mean_ref[...] = exact(own_ref[ns:, :] + exact(later_ref[ns:, :], whole), mixed, NT)[:1, :]


KERNEL_VMEM = 16 * 2**20
ALL_VMEM = 67 * 10**6
VMEM = pl.BlockSpec(memory_space=pltpu.VMEM)
HBM = pl.BlockSpec(memory_space=pltpu.MemorySpace.HBM)
SMEM = pl.BlockSpec(memory_space=pltpu.SMEM)


def call(kernel, args, rows, scratch, work, name, far=(), room=KERNEL_VMEM, **params):
    width = args[-1].shape[-1]
    read = sum(a.size for a in args) * 4
    return pl.pallas_call(
        kernel,
        out_shape=tuple(jax.ShapeDtypeStruct((r, width), F32) for r in rows),
        in_specs=[
            HBM if i in far else SMEM if a.ndim == 1 else VMEM for i, a in enumerate(args)
        ],
        out_specs=tuple(VMEM for _ in rows),
        scratch_shapes=scratch,
        cost_estimate=pl.CostEstimate(flops=work, bytes_accessed=read, transcendentals=0),
        compiler_params=pltpu.CompilerParams(vmem_limit_bytes=room, **params),
        name=name,
    )(*args)


def shards(measurements, noise_levels, transition, sensing, process_noise, prior_mean, prior_covariance):
    ns = transition.shape[0]
    no = sensing.shape[0]
    count = lax.axis_size("tm")
    device = lax.axis_index("tm").astype(jnp.int32)
    place = device.reshape(1)
    half = ns // 2 + 8
    tall = ns + 8
    work = 2 * ns**3 * 60

    def rows(r, columns=ns):
        return pltpu.VMEM((r, columns), F32)

    pair = rows(3 * ns)
    mine = jnp.concatenate([measurements, noise_levels], axis=0)
    other = lax.ppermute(mine, "tm", [(i, i ^ 1) for i in range(count)])
    def resolved(x, y):
        return call(resolve_kernel, (x, y), (tall,), [pair], work, "resolve")[0]

    leaves, x, y = call(
        start_kernel,
        (
            place,
            mine,
            other,
            transition,
            sensing,
            process_noise,
            prior_mean.reshape(1, ns),
            prior_covariance,
        ),
        (2 * (2 * tall + ns), tall, tall),
        [
            rows(ns),
            rows(no),
            rows(ns),
            rows(ns),
            rows(8),
            rows(no),
            rows(no),
            rows(no, no),
            rows(3 * no, no),
            pltpu.SemaphoreType.DMA((4,)),
        ],
        work,
        "start",
        far=(3, 4, 5, 7),
        room=ALL_VMEM,
    )
    s, moved, bound, y, message = call(
        pair_kernel,
        (place, resolved(x, y), leaves),
        (tall, ns, half, tall, half),
        [rows(tall)],
        work // 3,
        "pair",
    )
    (x,) = call(
        functools.partial(shift_kernel, 2, count),
        (message, s),
        (tall,),
        [rows(half), pltpu.SemaphoreType.DMA, pltpu.SemaphoreType.DMA],
        work // 60,
        "shift",
        collective_id=1,
        has_side_effects=True,
    )
    hop = 2
    while hop < count:
        last = hop * 2 >= count
        small = (8, 8) if last else (ns, half)
        spread_hop = 2 if last else 2 * hop
        solved = resolved(x, y)
        x, y, s, moved, bound = call(
            functools.partial(exchange_kernel, hop, spread_hop, count, last),
            (solved, x, y, s, moved, bound),
            (tall, tall, tall) + small,
            [
                rows(tall),
                rows(tall),
                rows(half),
                rows(half),
                rows(ns),
                rows(half),
                rows(half),
                rows(half),
                pltpu.SemaphoreType.DMA((7,)),
                pltpu.SemaphoreType.DMA((4,)),
            ],
            work,
            f"exchange_{hop}",
            collective_id=hop.bit_length(),
            has_side_effects=True,
        )
        hop *= 2
    left, right = call(choose_kernel, (place, x, y, leaves), (tall, tall), [], work // 60, "choose")
    solved = resolved(left, right)
    own, later = call(
        functools.partial(finish_kernel, count),
        (solved, x, y, leaves),
        (tall, tall),
        [rows(tall), rows(half), rows(half), pltpu.SemaphoreType.DMA, pltpu.SemaphoreType.DMA],
        work,
        "finish",
        collective_id=0,
        has_side_effects=True,
    )
    mean, cov = call(last_kernel, (resolved(own, later), own, later), (1, ns), [], work // 20, "last")
    return (mean, cov[None])


def solution(mesh):
    return jax.shard_map(
        shards,
        mesh=mesh,
        in_specs=(P("tm", None), P("tm", None), P(), P(), P(), P(), P()),
        out_specs=(P("tm", None), P("tm", None, None)),
        check_vma=False,
    )
```

profile of v0, /device:TPU:1, one launch (start us, length us, event | category | flops | bytes accessed | tf_op | source)
XLA Modules:
  0.0 162.3 jit_solution(15699145632891280812)
XLA Ops:
  0.6 0.7 pad_maximum_fusion.mine_ref
  1.3 0.0 copy-start.3
  1.3 3.3 %collective-permute-start = (f32[2,128]{1,0:T(2,128)S(1)}, f32[2,128]{1,0:T(2,128)S(1)}, u32[]{:S(2)}, u32[]{:S(2)}) collective-permute-start(f32[2,128]{1,0:T(2,128)S(1)} %pad_maximum_fusion.mine_ref), channel_id=1, source_target_pairs={{0,1},{1,0},{2,3},{3,2},{4,5},{5,4},{6,7},{7,6},{8,9},{9,8},{10,11... | collective-permute-start | bytes 3080 | tf_op jit(solution)/shard_map/ppermute | solution.py:589
  4.6 0.8 collective-permute-done.other_ref
  5.4 0.0 copy-start.4
  5.4 0.0 copy-done.3
  5.4 0.6 copy-done.4
  6.0 12.6 %start.1 = (f32[1568,256]{1,0:T(8,128)}, f32[264,256]{1,0:T(8,128)}, f32[264,256]{1,0:T(8,128)}) custom-call(s32[1]{0:T(128)} %bitcast.place_ref, f32[2,128]{1,0:T(2,128)} %copy-done.3, f32[2,128]{1,0:T(2,128)} %copy-done.4, f32[256,256]{1,0:T(8,128)} %f_hbm.1, f32[128,256]{1,0:T(8,128)} %h_hbm.1, f32[256,256]{1,0:T(8,128)} %q_hbm.1, f32[1,256]{1,0:T(1,128)} %bitcast.4, ...), custom_call_target="tpu_custom_call" | custom-call | flops 2013265920 | bytes 920580 | tf_op jit(solution)/shard_map/start/pallas_call | solution.py:560
  18.6 0.0 copy-start.1
  18.6 0.9 copy-done.1
  19.5 0.0 copy-start.2
  19.5 1.0 copy-done.2
  20.5 0.0 copy-start
  20.5 2.3 %resolve.10.solved = f32[264,256]{1,0:T(8,128)S(1)} custom-call(f32[264,256]{1,0:T(8,128)S(1)} %copy-done.1, f32[264,256]{1,0:T(8,128)S(1)} %copy-done.2), custom_call_target="tpu_custom_call" | custom-call | flops 2013265920 | bytes 540672 | tf_op jit(solution)/shard_map/resolve/pallas_call | solution.py:560
  22.8 0.0 copy-done
  22.8 2.2 %pair.1 = (f32[264,256]{1,0:T(8,128)S(1)}, f32[256,256]{1,0:T(8,128)S(1)}, f32[136,256]{1,0:T(8,128)S(1)}, f32[264,256]{1,0:T(8,128)S(1)}, f32[136,256]{1,0:T(8,128)S(1)}) custom-call(s32[1]{0:T(128)} %bitcast.place_ref, f32[264,256]{1,0:T(8,128)S(1)} %resolve.10.solved, f32[1568,256]{1,0:T(8,128)S(1)} %copy-done), custom_call_target="tpu_custom_call" | custom-call | flops 671088640 | bytes 1875972 | tf_op jit(solution)/shard_map/pair/pallas_call | solution.py:560
  25.0 0.2 shift.1.x_ref
  25.2 2.0 %resolve.11.solved = f32[264,256]{1,0:T(8,128)S(1)} custom-call(f32[264,256]{1,0:T(8,128)S(1)} %shift.1.x_ref, f32[264,256]{1,0:T(8,128)S(1)} %get-tuple-element.53.y_ref), custom_call_target="tpu_custom_call" | custom-call | flops 2013265920 | bytes 540672 | tf_op jit(solution)/shard_map/resolve/pallas_call | solution.py:560
  27.2 13.0 %exchange_2.1 = (f32[264,256]{1,0:T(8,128)S(1)}, f32[264,256]{1,0:T(8,128)S(1)}, f32[264,256]{1,0:T(8,128)S(1)}, f32[256,256]{1,0:T(8,128)S(1)}, f32[136,256]{1,0:T(8,128)S(1)}) custom-call(f32[264,256]{1,0:T(8,128)S(1)} %resolve.11.solved, f32[264,256]{1,0:T(8,128)S(1)} %shift.1.x_ref, f32[264,256]{1,0:T(8,128)S(1)} %get-tuple-element.53.y_ref, ...), custom_call_target="tpu_custom_call" | custom-call | flops 2013265920 | bytes 1482752 | tf_op jit(solution)/shard_map/exchange_2/pallas_call | solution.py:560
  40.2 2.3 %resolve.12.solved = f32[264,256]{1,0:T(8,128)S(1)} custom-call(f32[264,256]{1,0:T(8,128)S(1)} %get-tuple-element.56.x_ref, f32[264,256]{1,0:T(8,128)S(1)} %get-tuple-element.57.y_ref), custom_call_target="tpu_custom_call" | custom-call | flops 2013265920 | bytes 540672 | tf_op jit(solution)/shard_map/resolve/pallas_call | solution.py:560
  42.5 12.5 %exchange_4.1 = (f32[264,256]{1,0:T(8,128)S(1)}, f32[264,256]{1,0:T(8,128)S(1)}, f32[264,256]{1,0:T(8,128)S(1)}, f32[256,256]{1,0:T(8,128)S(1)}, f32[136,256]{1,0:T(8,128)S(1)}) custom-call(f32[264,256]{1,0:T(8,128)S(1)} %resolve.12.solved, f32[264,256]{1,0:T(8,128)S(1)} %get-tuple-element.56.x_ref, f32[264,256]{1,0:T(8,128)S(1)} %get-tuple-element.57.y_ref, ...), custom_call_target="tpu_custom_call" | custom-call | flops 2013265920 | bytes 1482752 | tf_op jit(solution)/shard_map/exchange_4/pallas_call | solution.py:560
  55.0 2.6 %resolve.13.solved = f32[264,256]{1,0:T(8,128)S(1)} custom-call(f32[264,256]{1,0:T(8,128)S(1)} %get-tuple-element.61.x_ref, f32[264,256]{1,0:T(8,128)S(1)} %get-tuple-element.62.y_ref), custom_call_target="tpu_custom_call" | custom-call | flops 2013265920 | bytes 540672 | tf_op jit(solution)/shard_map/resolve/pallas_call | solution.py:560
  57.6 12.3 %exchange_8.1 = (f32[264,256]{1,0:T(8,128)S(1)}, f32[264,256]{1,0:T(8,128)S(1)}, f32[264,256]{1,0:T(8,128)S(1)}, f32[256,256]{1,0:T(8,128)S(1)}, f32[136,256]{1,0:T(8,128)S(1)}) custom-call(f32[264,256]{1,0:T(8,128)S(1)} %resolve.13.solved, f32[264,256]{1,0:T(8,128)S(1)} %get-tuple-element.61.x_ref, f32[264,256]{1,0:T(8,128)S(1)} %get-tuple-element.62.y_ref, ...), custom_call_target="tpu_custom_call" | custom-call | flops 2013265920 | bytes 1482752 | tf_op jit(solution)/shard_map/exchange_8/pallas_call | solution.py:560
  69.9 2.6 %resolve.14.solved = f32[264,256]{1,0:T(8,128)S(1)} custom-call(f32[264,256]{1,0:T(8,128)S(1)} %get-tuple-element.66.x_ref, f32[264,256]{1,0:T(8,128)S(1)} %get-tuple-element.67.y_ref), custom_call_target="tpu_custom_call" | custom-call | flops 2013265920 | bytes 540672 | tf_op jit(solution)/shard_map/resolve/pallas_call | solution.py:560
  72.5 22.5 %exchange_16.1 = (f32[264,256]{1,0:T(8,128)S(1)}, f32[264,256]{1,0:T(8,128)S(1)}, f32[264,256]{1,0:T(8,128)S(1)}, f32[256,256]{1,0:T(8,128)S(1)}, f32[136,256]{1,0:T(8,128)S(1)}) custom-call(f32[264,256]{1,0:T(8,128)S(1)} %resolve.14.solved, f32[264,256]{1,0:T(8,128)S(1)} %get-tuple-element.66.x_ref, f32[264,256]{1,0:T(8,128)S(1)} %get-tuple-element.67.y_ref, ...), custom_call_target="tpu_custom_call" | custom-call | flops 2013265920 | bytes 1482752 | tf_op jit(solution)/shard_map/exchange_16/pallas_call | solution.py:560
  94.9 2.9 %resolve.15.solved = f32[264,256]{1,0:T(8,128)S(1)} custom-call(f32[264,256]{1,0:T(8,128)S(1)} %get-tuple-element.71.x_ref, f32[264,256]{1,0:T(8,128)S(1)} %get-tuple-element.72.y_ref), custom_call_target="tpu_custom_call" | custom-call | flops 2013265920 | bytes 540672 | tf_op jit(solution)/shard_map/resolve/pallas_call | solution.py:560
  97.8 23.9 %exchange_32.1 = (f32[264,256]{1,0:T(8,128)S(1)}, f32[264,256]{1,0:T(8,128)S(1)}, f32[264,256]{1,0:T(8,128)S(1)}, f32[256,256]{1,0:T(8,128)S(1)}, f32[136,256]{1,0:T(8,128)S(1)}) custom-call(f32[264,256]{1,0:T(8,128)S(1)} %resolve.15.solved, f32[264,256]{1,0:T(8,128)S(1)} %get-tuple-element.71.x_ref, f32[264,256]{1,0:T(8,128)S(1)} %get-tuple-element.72.y_ref, ...), custom_call_target="tpu_custom_call" | custom-call | flops 2013265920 | bytes 1482752 | tf_op jit(solution)/shard_map/exchange_32/pallas_call | solution.py:560
  121.7 2.9 %resolve.16.solved = f32[264,256]{1,0:T(8,128)S(1)} custom-call(f32[264,256]{1,0:T(8,128)S(1)} %get-tuple-element.76.x_ref, f32[264,256]{1,0:T(8,128)S(1)} %get-tuple-element.77.y_ref), custom_call_target="tpu_custom_call" | custom-call | flops 2013265920 | bytes 540672 | tf_op jit(solution)/shard_map/resolve/pallas_call | solution.py:560
  124.5 13.5 %exchange_64.1 = (f32[264,256]{1,0:T(8,128)S(1)}, f32[264,256]{1,0:T(8,128)S(1)}, f32[264,256]{1,0:T(8,128)S(1)}, f32[256,256]{1,0:T(8,128)S(1)}, f32[136,256]{1,0:T(8,128)S(1)}) custom-call(f32[264,256]{1,0:T(8,128)S(1)} %resolve.16.solved, f32[264,256]{1,0:T(8,128)S(1)} %get-tuple-element.76.x_ref, f32[264,256]{1,0:T(8,128)S(1)} %get-tuple-element.77.y_ref, ...), custom_call_target="tpu_custom_call" | custom-call | flops 2013265920 | bytes 1482752 | tf_op jit(solution)/shard_map/exchange_64/pallas_call | solution.py:560
  138.0 2.9 %resolve.17.solved = f32[264,256]{1,0:T(8,128)S(1)} custom-call(f32[264,256]{1,0:T(8,128)S(1)} %get-tuple-element.81.x_ref, f32[264,256]{1,0:T(8,128)S(1)} %get-tuple-element.82.y_ref), custom_call_target="tpu_custom_call" | custom-call | flops 2013265920 | bytes 540672 | tf_op jit(solution)/shard_map/resolve/pallas_call | solution.py:560
  140.9 12.6 %exchange_128.1 = (f32[264,256]{1,0:T(8,128)S(1)}, f32[264,256]{1,0:T(8,128)S(1)}, f32[264,256]{1,0:T(8,128)}, f32[8,256]{1,0:T(8,128)}, f32[8,256]{1,0:T(8,128)}) custom-call(f32[264,256]{1,0:T(8,128)S(1)} %resolve.17.solved, f32[264,256]{1,0:T(8,128)S(1)} %get-tuple-element.81.x_ref, f32[264,256]{1,0:T(8,128)S(1)} %get-tuple-element.82.y_ref, ...), custom_call_target="tpu_custom_call" | custom-call | flops 2013265920 | bytes 1482752 | tf_op jit(solution)/shard_map/exchange_128/pallas_call | solution.py:560
  153.5 2.3 %resolve.18.solved = f32[264,256]{1,0:T(8,128)S(1)} custom-call(f32[264,256]{1,0:T(8,128)S(1)} %get-tuple-element.88.x_ref, f32[264,256]{1,0:T(8,128)S(1)} %get-tuple-element.89.y_ref), custom_call_target="tpu_custom_call" | custom-call | flops 2013265920 | bytes 540672 | tf_op jit(solution)/shard_map/resolve/pallas_call | solution.py:560
  155.8 2.1 %finish.1 = (f32[264,256]{1,0:T(8,128)S(1)}, f32[264,256]{1,0:T(8,128)S(1)}) custom-call(f32[264,256]{1,0:T(8,128)S(1)} %resolve.18.solved, f32[264,256]{1,0:T(8,128)S(1)} %get-tuple-element.86.x_ref, f32[264,256]{1,0:T(8,128)S(1)} %get-tuple-element.87.y_ref, f32[1568,256]{1,0:T(8,128)S(1)} %copy-done), custom_call_target="tpu_custom_call" | custom-call | flops 2013265920 | bytes 2416640 | tf_op jit(solution)/shard_map/finish/pallas_call | solution.py:560
  157.9 2.8 %resolve.19.solved = f32[264,256]{1,0:T(8,128)S(1)} custom-call(f32[264,256]{1,0:T(8,128)S(1)} %get-tuple-element.90.x_ref.own_ref, f32[264,256]{1,0:T(8,128)S(1)} %get-tuple-element.91.y_ref.later_ref), custom_call_target="tpu_custom_call" | custom-call | flops 2013265920 | bytes 540672 | tf_op jit(solution)/shard_map/resolve/pallas_call | solution.py:560
  160.8 1.5 last.1
  (1 shorter events, 0.0 us)
Async XLA Ops:
  1.3 4.1 %copy-start.3 = (f32[2,128]{1,0:T(2,128)}, f32[2,128]{1,0:T(2,128)S(1)}, u32[]{:S(2)}) copy-start(f32[2,128]{1,0:T(2,128)S(1)} %pad_maximum_fusion.mine_ref) | copy-start | bytes 3076
  1.3 4.1 %collective-permute-start = (f32[2,128]{1,0:T(2,128)S(1)}, f32[2,128]{1,0:T(2,128)S(1)}, u32[]{:S(2)}, u32[]{:S(2)}) collective-permute-start(f32[2,128]{1,0:T(2,128)S(1)} %pad_maximum_fusion.mine_ref), channel_id=1, source_target_pairs={{0,1},{1,0},{2,3},{3,2},{4,5},{5,4},{6,7},{7,6},{8,9},{9,8},{10,11... | collective-permute-start | bytes 3080 | tf_op jit(solution)/shard_map/ppermute | solution.py:589
  5.4 0.6 copy-start.4
  18.6 1.0 copy-start.1
  19.5 1.0 copy-start.2
  20.5 2.3 %copy-start = (f32[1568,256]{1,0:T(8,128)S(1)}, f32[1568,256]{1,0:T(8,128)}, u32[]{:S(2)}) copy-start(f32[1568,256]{1,0:T(8,128)} %get-tuple-element.50.leaves) | copy-start | bytes 4816900
where the time goes:
time: 162 us
  Pallas kernels  154 us (95%)
  starting transfers between devices  3.28 us (2%)
  local copies, waits for them, and re-layouts  2.46 us (2%)
    pallas_call x23, Pallas kernels, call(): pl.pallas_call(kernel, out_shape=tuple((jax.ShapeDtypeStruct((r, width),...  154 us
    ppermute x1, starting transfers between devices, shards(): other = lax.ppermute(mine, 'tm', [(i, i ^ 1) for i in range(count)])  3.28 us
  transfers between devices with their start and end apart: 1, of which 1 were waited for; matrix products, arithmetic and copies ran while one was open for 0% of the time, Pallas kernels for 0%

commit v1 on v0

--- a/solution.py
+++ b/solution.py
@@ -176,8 +176,8 @@
 
 def start_kernel(
     place_ref, mine_ref, other_ref, f_hbm, h_hbm, q_hbm, m_ref, p_hbm,
-    leaves, x_out, y_out,
-    f_ref, h_ref, noise, p_ref, center, plain, sensed_plain, inner_plain, half_pair, sems,
+    leaves, solved,
+    f_ref, h_ref, noise, p_ref, center, plain, sensed_plain, inner_plain, half_pair, pair, sems,
 ):
     chip, core = lax.div(place_ref[0], 2), lax.rem(place_ref[0], 2)
     lead = core == 0
@@ -236,33 +236,9 @@
         return carry
 
     lax.fori_loop(0, 2, leaf, 0)
-    x_out[...] = leaves[size + ns : size + ns + tall, :]
-    y_out[...] = leaves[ns + tall : size, :]
-
-
-def pair_kernel(
-    place_ref, solved, leaves, s_out, move_out, bind_out, y_out, spread_msg, through
-):
-    ns = solved.shape[1]
-    tall = ns + 8
-    size = 2 * tall + ns
-    odd, even = leaves.at[:size, :], leaves.at[size:, :]
-    lead = lax.rem(place_ref[0], 2) == 0
-    x_ref = even.at[ns : ns + tall, :]
-    y_ref = odd.at[ns + tall :, :]
-    later = odd[:ns, :]
-    early = even[:ns, :]
-    fill(through, exact(later, solved[:ns, :]), y_ref[ns:, :])
-    later_spread(through, x_ref, later, odd.at[ns : ns + tall, :], s_out)
-    pack(spread_msg, s_out[:ns, :], s_out[ns:, :])
-    move_out[...] = exact(through[:ns, :], early)
-    fill(through, y_ref[:ns, :], solved[ns:, :])
-    both = medium(medium(through[...], solved[:ns, :]), early)
-    bind = medium(early.T, both[:ns, :]) + even[ns + tall : ns + tall + ns, :]
-    pull = both[ns:, :] + even[2 * ns + tall :, :]
-    pack(bind_out, bind, pull)
-    scale = jnp.where(lead, 1.0, 0.0)
-    fill(y_out, scale * bind, scale * pull)
+    resolve(
+        leaves.at[size + ns : size + ns + tall, :], leaves.at[ns + tall : size, :], solved, pair
+    )
 
 
 def resolve_kernel(x_ref, y_ref, out, pair):
@@ -292,7 +268,14 @@
     return arrive
 
 
-def shift_kernel(hop, count, message, s_ref, x_out, land, send_sem, recv_sem):
+def pair_kernel(
+    hop, count,
+    solved, leaves, x_out, y_out, s_out, move_out, bind_out,
+    through, message, land, send_sem, recv_sem,
+):
+    ns = solved.shape[1]
+    tall = ns + 8
+    size = 2 * tall + ns
     mine = lax.axis_index("tm")
     lead = lax.rem(mine, 2) == 0
     side = jnp.logical_not(lead)
@@ -307,12 +290,31 @@
     )
     sends = jnp.logical_and(lead, mine + hop < count)
     takes = jnp.logical_and(lead, mine - hop >= 0)
+    odd, even = leaves.at[:size, :], leaves.at[size:, :]
+    x_ref = even.at[ns : ns + tall, :]
+    y_ref = odd.at[ns + tall :, :]
+    later = odd[:ns, :]
+    early = even[:ns, :]
+    fill(through, exact(later, solved[:ns, :]), y_ref[ns:, :])
+    later_spread(through, x_ref, later, odd.at[ns : ns + tall, :], s_out)
+    pack(message, s_out[:ns, :], s_out[ns:, :])
     arrive()
     pl.when(sends)(copy.start)
+    move_out[...] = exact(through[:ns, :], early)
+    fill(through, y_ref[:ns, :], solved[ns:, :])
+    both = medium(medium(through[...], solved[:ns, :]), early)
+    bind = medium(early.T, both[:ns, :]) + even[ns + tall : ns + tall + ns, :]
+    pull = both[ns:, :] + even[2 * ns + tall :, :]
+    pack(bind_out, bind, pull)
+
+    @pl.when(lead)
+    def _():
+        fill(y_out, bind, pull)
 
     @pl.when(side)
     def _():
-        x_out[...] = s_ref[...]
+        y_out[...] = jnp.zeros_like(y_out)
+        x_out[...] = s_out[...]
 
     @pl.when(jnp.logical_and(lead, mine - hop < 0))
     def _():
@@ -377,7 +379,7 @@
     def _():
         fill(through, exact(move_ref[...], solved[:ns, :]), y_ref[ns:, :])
 
-    arrive()
+    pl.when(lead)(arrive)
     if not last:
 
         @pl.when(move_sends)
@@ -433,6 +435,7 @@
         pl.when(side)(rest)
     else:
         rest()
+    pl.when(side)(arrive)
     pl.when(bind_sends)(bind_down.start)
     if not last:
 
@@ -590,7 +593,7 @@
     def resolved(x, y):
         return call(resolve_kernel, (x, y), (tall,), [pair], work, "resolve")[0]
 
-    leaves, x, y = call(
+    leaves, solved = call(
         start_kernel,
         (
             place,
@@ -602,7 +605,7 @@
             prior_mean.reshape(1, ns),
             prior_covariance,
         ),
-        (2 * (2 * tall + ns), tall, tall),
+        (2 * (2 * tall + ns), tall),
         [
             rows(ns),
             rows(no),
@@ -613,6 +616,7 @@
             rows(no),
             rows(no, no),
             rows(3 * no, no),
+            pair,
             pltpu.SemaphoreType.DMA((4,)),
         ],
         work,
@@ -620,21 +624,13 @@
         far=(3, 4, 5, 7),
         room=ALL_VMEM,
     )
-    s, moved, bound, y, message = call(
-        pair_kernel,
-        (place, resolved(x, y), leaves),
-        (tall, ns, half, tall, half),
-        [rows(tall)],
+    x, y, s, moved, bound = call(
+        functools.partial(pair_kernel, 2, count),
+        (solved, leaves),
+        (tall, tall, tall, ns, half),
+        [rows(tall), rows(half), rows(half), pltpu.SemaphoreType.DMA, pltpu.SemaphoreType.DMA],
         work // 3,
         "pair",
-    )
-    (x,) = call(
-        functools.partial(shift_kernel, 2, count),
-        (message, s),
-        (tall,),
-        [rows(half), pltpu.SemaphoreType.DMA, pltpu.SemaphoreType.DMA],
-        work // 60,
-        "shift",
         collective_id=1,
         has_side_effects=True,
     )

time: 162 us -> 161 us (level)
  Pallas kernels: 154 us -> 152 us
    pallas_call x23 -> x21, Pallas kernels: 154 us -> 152 us  [call(): pl.pallas_call(kernel, out_shape=tuple((jax.ShapeDtypeStruct((r, width),...]
where the time goes in v1:
time: 161 us; the launch traced here: 160 us
  Pallas kernels  152 us (94%)
  starting transfers between devices  3.28 us (2%)
  local copies, waits for them, and re-layouts  2.93 us (2%)
    pallas_call x21, Pallas kernels, call(): pl.pallas_call(kernel, out_shape=tuple((jax.ShapeDtypeStruct((r, width),...  152 us
    ppermute x1, starting transfers between devices, shards(): other = lax.ppermute(mine, 'tm', [(i, i ^ 1) for i in range(count)])  3.28 us
  transfers between devices with their start and end apart: 1, of which 1 were waited for; matrix products, arithmetic and copies ran while one was open for 0% of the time, Pallas kernels for 0%

profile of v1, /device:TPU:1, one launch (start us, length us, event | category | flops | bytes accessed | tf_op | source)
XLA Modules:
  0.0 160.3 jit_solution(2756605549445816375)
XLA Ops:
  0.6 0.7 pad_maximum_fusion.mine_ref
  1.3 0.0 copy-start.3
  1.3 3.3 %collective-permute-start = (f32[2,128]{1,0:T(2,128)S(1)}, f32[2,128]{1,0:T(2,128)S(1)}, u32[]{:S(2)}, u32[]{:S(2)}) collective-permute-start(f32[2,128]{1,0:T(2,128)S(1)} %pad_maximum_fusion.mine_ref), channel_id=1, source_target_pairs={{0,1},{1,0},{2,3},{3,2},{4,5},{5,4},{6,7},{7,6},{8,9},{9,8},{10,11... | collective-permute-start | bytes 3080 | tf_op jit(solution)/shard_map/ppermute | solution.py:592
  4.6 0.8 collective-permute-done.other_ref
  5.4 0.0 copy-start.4
  5.4 0.0 copy-done.3
  5.4 0.6 copy-done.4
  6.0 14.3 %start.1 = (f32[1568,256]{1,0:T(8,128)}, f32[264,256]{1,0:T(8,128)}) custom-call(s32[1]{0:T(128)} %bitcast.place_ref, f32[2,128]{1,0:T(2,128)} %copy-done.3, f32[2,128]{1,0:T(2,128)} %copy-done.4, f32[256,256]{1,0:T(8,128)} %f_hbm.1, f32[128,256]{1,0:T(8,128)} %h_hbm.1, f32[256,256]{1,0:T(8,128)} %q_hbm.1, f32[1,256]{1,0:T(1,128)} %bitcast.4, f32[256,256]{1,0:T(8,128)} %p_hbm.1), custom_call_target="tpu_custom_call" | custom-call | flops 2013265920 | bytes 920580 | tf_op jit(solution)/shard_map/start/pallas_call | solution.py:563
  20.3 0.0 copy-start
  20.3 1.4 copy-done
  21.7 0.0 copy-start.2
  21.7 1.0 copy-done.2
  22.7 2.6 %pair.1 = (f32[264,256]{1,0:T(8,128)S(1)}, f32[264,256]{1,0:T(8,128)S(1)}, f32[264,256]{1,0:T(8,128)S(1)}, f32[256,256]{1,0:T(8,128)S(1)}, f32[136,256]{1,0:T(8,128)S(1)}) custom-call(f32[264,256]{1,0:T(8,128)S(1)} %copy-done.2, f32[1568,256]{1,0:T(8,128)S(1)} %copy-done), custom_call_target="tpu_custom_call" | custom-call | flops 671088640 | bytes 1875968 | tf_op jit(solution)/shard_map/pair/pallas_call | solution.py:563
  25.3 2.0 %resolve.9.solved = f32[264,256]{1,0:T(8,128)S(1)} custom-call(f32[264,256]{1,0:T(8,128)S(1)} %get-tuple-element.49.x_ref, f32[264,256]{1,0:T(8,128)S(1)} %get-tuple-element.50.y_ref), custom_call_target="tpu_custom_call" | custom-call | flops 2013265920 | bytes 540672 | tf_op jit(solution)/shard_map/resolve/pallas_call | solution.py:563
  27.3 10.4 %exchange_2.1 = (f32[264,256]{1,0:T(8,128)S(1)}, f32[264,256]{1,0:T(8,128)S(1)}, f32[264,256]{1,0:T(8,128)S(1)}, f32[256,256]{1,0:T(8,128)S(1)}, f32[136,256]{1,0:T(8,128)S(1)}) custom-call(f32[264,256]{1,0:T(8,128)S(1)} %resolve.9.solved, f32[264,256]{1,0:T(8,128)S(1)} %get-tuple-element.49.x_ref, f32[264,256]{1,0:T(8,128)S(1)} %get-tuple-element.50.y_ref, ...), custom_call_target="tpu_custom_call" | custom-call | flops 2013265920 | bytes 1482752 | tf_op jit(solution)/shard_map/exchange_2/pallas_call | solution.py:563
  37.8 2.3 %resolve.10.solved = f32[264,256]{1,0:T(8,128)S(1)} custom-call(f32[264,256]{1,0:T(8,128)S(1)} %get-tuple-element.54.x_ref, f32[264,256]{1,0:T(8,128)S(1)} %get-tuple-element.55.y_ref), custom_call_target="tpu_custom_call" | custom-call | flops 2013265920 | bytes 540672 | tf_op jit(solution)/shard_map/resolve/pallas_call | solution.py:563
  40.1 13.8 %exchange_4.1 = (f32[264,256]{1,0:T(8,128)S(1)}, f32[264,256]{1,0:T(8,128)S(1)}, f32[264,256]{1,0:T(8,128)S(1)}, f32[256,256]{1,0:T(8,128)S(1)}, f32[136,256]{1,0:T(8,128)S(1)}) custom-call(f32[264,256]{1,0:T(8,128)S(1)} %resolve.10.solved, f32[264,256]{1,0:T(8,128)S(1)} %get-tuple-element.54.x_ref, f32[264,256]{1,0:T(8,128)S(1)} %get-tuple-element.55.y_ref, ...), custom_call_target="tpu_custom_call" | custom-call | flops 2013265920 | bytes 1482752 | tf_op jit(solution)/shard_map/exchange_4/pallas_call | solution.py:563
  53.8 2.6 %resolve.11.solved = f32[264,256]{1,0:T(8,128)S(1)} custom-call(f32[264,256]{1,0:T(8,128)S(1)} %get-tuple-element.59.x_ref, f32[264,256]{1,0:T(8,128)S(1)} %get-tuple-element.60.y_ref), custom_call_target="tpu_custom_call" | custom-call | flops 2013265920 | bytes 540672 | tf_op jit(solution)/shard_map/resolve/pallas_call | solution.py:563
  56.4 11.3 %exchange_8.1 = (f32[264,256]{1,0:T(8,128)S(1)}, f32[264,256]{1,0:T(8,128)S(1)}, f32[264,256]{1,0:T(8,128)S(1)}, f32[256,256]{1,0:T(8,128)S(1)}, f32[136,256]{1,0:T(8,128)S(1)}) custom-call(f32[264,256]{1,0:T(8,128)S(1)} %resolve.11.solved, f32[264,256]{1,0:T(8,128)S(1)} %get-tuple-element.59.x_ref, f32[264,256]{1,0:T(8,128)S(1)} %get-tuple-element.60.y_ref, ...), custom_call_target="tpu_custom_call" | custom-call | flops 2013265920 | bytes 1482752 | tf_op jit(solution)/shard_map/exchange_8/pallas_call | solution.py:563
  67.7 2.6 %resolve.12.solved = f32[264,256]{1,0:T(8,128)S(1)} custom-call(f32[264,256]{1,0:T(8,128)S(1)} %get-tuple-element.64.x_ref, f32[264,256]{1,0:T(8,128)S(1)} %get-tuple-element.65.y_ref), custom_call_target="tpu_custom_call" | custom-call | flops 2013265920 | bytes 540672 | tf_op jit(solution)/shard_map/resolve/pallas_call | solution.py:563
  70.3 22.5 %exchange_16.1 = (f32[264,256]{1,0:T(8,128)S(1)}, f32[264,256]{1,0:T(8,128)S(1)}, f32[264,256]{1,0:T(8,128)S(1)}, f32[256,256]{1,0:T(8,128)S(1)}, f32[136,256]{1,0:T(8,128)S(1)}) custom-call(f32[264,256]{1,0:T(8,128)S(1)} %resolve.12.solved, f32[264,256]{1,0:T(8,128)S(1)} %get-tuple-element.64.x_ref, f32[264,256]{1,0:T(8,128)S(1)} %get-tuple-element.65.y_ref, ...), custom_call_target="tpu_custom_call" | custom-call | flops 2013265920 | bytes 1482752 | tf_op jit(solution)/shard_map/exchange_16/pallas_call | solution.py:563
  92.8 2.9 %resolve.13.solved = f32[264,256]{1,0:T(8,128)S(1)} custom-call(f32[264,256]{1,0:T(8,128)S(1)} %get-tuple-element.69.x_ref, f32[264,256]{1,0:T(8,128)S(1)} %get-tuple-element.70.y_ref), custom_call_target="tpu_custom_call" | custom-call | flops 2013265920 | bytes 540672 | tf_op jit(solution)/shard_map/resolve/pallas_call | solution.py:563
  95.6 23.8 %exchange_32.1 = (f32[264,256]{1,0:T(8,128)S(1)}, f32[264,256]{1,0:T(8,128)S(1)}, f32[264,256]{1,0:T(8,128)S(1)}, f32[256,256]{1,0:T(8,128)S(1)}, f32[136,256]{1,0:T(8,128)S(1)}) custom-call(f32[264,256]{1,0:T(8,128)S(1)} %resolve.13.solved, f32[264,256]{1,0:T(8,128)S(1)} %get-tuple-element.69.x_ref, f32[264,256]{1,0:T(8,128)S(1)} %get-tuple-element.70.y_ref, ...), custom_call_target="tpu_custom_call" | custom-call | flops 2013265920 | bytes 1482752 | tf_op jit(solution)/shard_map/exchange_32/pallas_call | solution.py:563
  119.4 3.1 %resolve.14.solved = f32[264,256]{1,0:T(8,128)S(1)} custom-call(f32[264,256]{1,0:T(8,128)S(1)} %get-tuple-element.74.x_ref, f32[264,256]{1,0:T(8,128)S(1)} %get-tuple-element.75.y_ref), custom_call_target="tpu_custom_call" | custom-call | flops 2013265920 | bytes 540672 | tf_op jit(solution)/shard_map/resolve/pallas_call | solution.py:563
  122.5 13.3 %exchange_64.1 = (f32[264,256]{1,0:T(8,128)S(1)}, f32[264,256]{1,0:T(8,128)S(1)}, f32[264,256]{1,0:T(8,128)S(1)}, f32[256,256]{1,0:T(8,128)S(1)}, f32[136,256]{1,0:T(8,128)S(1)}) custom-call(f32[264,256]{1,0:T(8,128)S(1)} %resolve.14.solved, f32[264,256]{1,0:T(8,128)S(1)} %get-tuple-element.74.x_ref, f32[264,256]{1,0:T(8,128)S(1)} %get-tuple-element.75.y_ref, ...), custom_call_target="tpu_custom_call" | custom-call | flops 2013265920 | bytes 1482752 | tf_op jit(solution)/shard_map/exchange_64/pallas_call | solution.py:563
  135.8 2.9 %resolve.15.solved = f32[264,256]{1,0:T(8,128)S(1)} custom-call(f32[264,256]{1,0:T(8,128)S(1)} %get-tuple-element.79.x_ref, f32[264,256]{1,0:T(8,128)S(1)} %get-tuple-element.80.y_ref), custom_call_target="tpu_custom_call" | custom-call | flops 2013265920 | bytes 540672 | tf_op jit(solution)/shard_map/resolve/pallas_call | solution.py:563
  138.7 0.0 copy-start.1
  138.7 12.7 %exchange_128.1 = (f32[264,256]{1,0:T(8,128)S(1)}, f32[264,256]{1,0:T(8,128)S(1)}, f32[264,256]{1,0:T(8,128)}, f32[8,256]{1,0:T(8,128)}, f32[8,256]{1,0:T(8,128)}) custom-call(f32[264,256]{1,0:T(8,128)S(1)} %resolve.15.solved, f32[264,256]{1,0:T(8,128)S(1)} %get-tuple-element.79.x_ref, f32[264,256]{1,0:T(8,128)S(1)} %get-tuple-element.80.y_ref, ...), custom_call_target="tpu_custom_call" | custom-call | flops 2013265920 | bytes 1482752 | tf_op jit(solution)/shard_map/exchange_128/pallas_call | solution.py:563
  151.4 0.0 copy-done.1
  151.5 2.3 %resolve.16.solved = f32[264,256]{1,0:T(8,128)S(1)} custom-call(f32[264,256]{1,0:T(8,128)S(1)} %get-tuple-element.86.x_ref, f32[264,256]{1,0:T(8,128)S(1)} %get-tuple-element.87.y_ref), custom_call_target="tpu_custom_call" | custom-call | flops 2013265920 | bytes 540672 | tf_op jit(solution)/shard_map/resolve/pallas_call | solution.py:563
  153.8 2.1 %finish.1 = (f32[264,256]{1,0:T(8,128)S(1)}, f32[264,256]{1,0:T(8,128)S(1)}) custom-call(f32[264,256]{1,0:T(8,128)S(1)} %resolve.16.solved, f32[264,256]{1,0:T(8,128)S(1)} %get-tuple-element.84.x_ref, f32[264,256]{1,0:T(8,128)S(1)} %get-tuple-element.85.y_ref, f32[1568,256]{1,0:T(8,128)S(1)} %copy-done.1), custom_call_target="tpu_custom_call" | custom-call | flops 2013265920 | bytes 2416640 | tf_op jit(solution)/shard_map/finish/pallas_call | solution.py:563
  155.9 2.9 %resolve.17.solved = f32[264,256]{1,0:T(8,128)S(1)} custom-call(f32[264,256]{1,0:T(8,128)S(1)} %get-tuple-element.88.x_ref.own_ref, f32[264,256]{1,0:T(8,128)S(1)} %get-tuple-element.89.y_ref.later_ref), custom_call_target="tpu_custom_call" | custom-call | flops 2013265920 | bytes 540672 | tf_op jit(solution)/shard_map/resolve/pallas_call | solution.py:563
  158.7 1.5 last.1
  (1 shorter events, 0.0 us)
Async XLA Ops:
  1.3 4.1 %copy-start.3 = (f32[2,128]{1,0:T(2,128)}, f32[2,128]{1,0:T(2,128)S(1)}, u32[]{:S(2)}) copy-start(f32[2,128]{1,0:T(2,128)S(1)} %pad_maximum_fusion.mine_ref) | copy-start | bytes 3076
  1.3 4.1 %collective-permute-start = (f32[2,128]{1,0:T(2,128)S(1)}, f32[2,128]{1,0:T(2,128)S(1)}, u32[]{:S(2)}, u32[]{:S(2)}) collective-permute-start(f32[2,128]{1,0:T(2,128)S(1)} %pad_maximum_fusion.mine_ref), channel_id=1, source_target_pairs={{0,1},{1,0},{2,3},{3,2},{4,5},{5,4},{6,7},{7,6},{8,9},{9,8},{10,11... | collective-permute-start | bytes 3080 | tf_op jit(solution)/shard_map/ppermute | solution.py:592
  5.4 0.6 copy-start.4
  20.3 1.4 copy-start
  21.7 1.0 copy-start.2
  138.7 12.7 %copy-start.1 = (f32[1568,256]{1,0:T(8,128)S(1)}, f32[1568,256]{1,0:T(8,128)}, u32[]{:S(2)}) copy-start(f32[1568,256]{1,0:T(8,128)} %get-tuple-element.48.leaves) | copy-start | bytes 4816900

commit v2 on v1

--- a/solution.py
+++ b/solution.py
@@ -176,7 +176,7 @@
 
 def start_kernel(
     place_ref, mine_ref, other_ref, f_hbm, h_hbm, q_hbm, m_ref, p_hbm,
-    leaves, solved,
+    leaves,
     f_ref, h_ref, noise, p_ref, center, plain, sensed_plain, inner_plain, half_pair, pair, sems,
 ):
     chip, core = lax.div(place_ref[0], 2), lax.rem(place_ref[0], 2)
@@ -237,7 +237,10 @@
 
     lax.fori_loop(0, 2, leaf, 0)
     resolve(
-        leaves.at[size + ns : size + ns + tall, :], leaves.at[ns + tall : size, :], solved, pair
+        leaves.at[size + ns : size + ns + tall, :],
+        leaves.at[ns + tall : size, :],
+        leaves.at[2 * size :, :],
+        pair,
     )
 
 
@@ -270,10 +273,10 @@
 
 def pair_kernel(
     hop, count,
-    solved, leaves, x_out, y_out, s_out, move_out, bind_out,
+    leaves, x_out, y_out, s_out, move_out, bind_out,
     through, message, land, send_sem, recv_sem,
 ):
-    ns = solved.shape[1]
+    ns = leaves.shape[1]
     tall = ns + 8
     size = 2 * tall + ns
     mine = lax.axis_index("tm")
@@ -290,7 +293,8 @@
     )
     sends = jnp.logical_and(lead, mine + hop < count)
     takes = jnp.logical_and(lead, mine - hop >= 0)
-    odd, even = leaves.at[:size, :], leaves.at[size:, :]
+    odd, even = leaves.at[:size, :], leaves.at[size : 2 * size, :]
+    solved = leaves.at[2 * size :, :]
     x_ref = even.at[ns : ns + tall, :]
     y_ref = odd.at[ns + tall :, :]
     later = odd[:ns, :]
@@ -375,10 +379,6 @@
         pull_up = carry(bind_ref, pull_land, 6, 1, hop)
         move_takes = jnp.logical_or(side, reaches(-hop))
 
-    @pl.when(lead)
-    def _():
-        fill(through, exact(move_ref[...], solved[:ns, :]), y_ref[ns:, :])
-
     pl.when(lead)(arrive)
     if not last:
 
@@ -391,6 +391,7 @@
     def _():
         move_side.start()
         pull_side.start()
+        fill(through, exact(move_ref[...], solved[:ns, :]), y_ref[ns:, :])
 
     def mix():
         fill(middle, y_ref[:ns, :], solved[ns:, :])
@@ -483,7 +484,7 @@
     ns = x_ref.shape[1]
     tall = ns + 8
     core = lax.rem(place_ref[0], 2)
-    odd, even = leaves.at[: 2 * tall + ns, :], leaves.at[2 * tall + ns :, :]
+    odd, even = leaves.at[: 2 * tall + ns, :], leaves.at[2 * tall + ns : 4 * tall + 2 * ns, :]
 
     @pl.when(core == 0)
     def _():
@@ -502,7 +503,7 @@
     mine = lax.axis_index("tm")
     lead = lax.rem(mine, 2) == 0
     side = jnp.logical_not(lead)
-    odd, even = leaves.at[: 2 * tall + ns, :], leaves.at[2 * tall + ns :, :]
+    odd, even = leaves.at[: 2 * tall + ns, :], leaves.at[2 * tall + ns : 4 * tall + 2 * ns, :]
     arrive = greet(mine, count, [(lead, 1), (side, -1)])
     copy = pltpu.make_async_remote_copy(
         src_ref=message,
@@ -593,7 +594,7 @@
     def resolved(x, y):
         return call(resolve_kernel, (x, y), (tall,), [pair], work, "resolve")[0]
 
-    leaves, solved = call(
+    (leaves,) = call(
         start_kernel,
         (
             place,
@@ -605,7 +606,7 @@
             prior_mean.reshape(1, ns),
             prior_covariance,
         ),
-        (2 * (2 * tall + ns), tall),
+        (5 * tall + 2 * ns,),
         [
             rows(ns),
             rows(no),
@@ -626,7 +627,7 @@
     )
     x, y, s, moved, bound = call(
         functools.partial(pair_kernel, 2, count),
-        (solved, leaves),
+        (leaves,),
         (tall, tall, tall, ns, half),
         [rows(tall), rows(half), rows(half), pltpu.SemaphoreType.DMA, pltpu.SemaphoreType.DMA],
         work // 3,

time: 161 us -> 160 us (level)
  no operation moved by 1% of the time
where the time goes in v2:
time: 160 us
  Pallas kernels  153 us (96%)
  starting transfers between devices  3.28 us (2%)
  local copies, waits for them, and re-layouts  2.07 us (1%)
    pallas_call x21, Pallas kernels, call(): pl.pallas_call(kernel, out_shape=tuple((jax.ShapeDtypeStruct((r, width),...  153 us
    ppermute x1, starting transfers between devices, shards(): other = lax.ppermute(mine, 'tm', [(i, i ^ 1) for i in range(count)])  3.28 us
  transfers between devices with their start and end apart: 1, of which 1 were waited for; matrix products, arithmetic and copies ran while one was open for 0% of the time, Pallas kernels for 0%

profile of v2, /device:TPU:1, one launch (start us, length us, event | category | flops | bytes accessed | tf_op | source)
XLA Modules:
  0.0 160.3 jit_solution(16186927451660600740)
XLA Ops:
  0.6 0.7 pad_maximum_fusion.mine_ref
  1.3 0.0 copy-start.2
  1.3 3.3 %collective-permute-start = (f32[2,128]{1,0:T(2,128)S(1)}, f32[2,128]{1,0:T(2,128)S(1)}, u32[]{:S(2)}, u32[]{:S(2)}) collective-permute-start(f32[2,128]{1,0:T(2,128)S(1)} %pad_maximum_fusion.mine_ref), channel_id=1, source_target_pairs={{0,1},{1,0},{2,3},{3,2},{4,5},{5,4},{6,7},{7,6},{8,9},{9,8},{10,11... | collective-permute-start | bytes 3080 | tf_op jit(solution)/shard_map/ppermute | solution.py:593
  4.6 0.8 collective-permute-done.other_ref
  5.4 0.0 copy-start.3
  5.4 0.0 copy-done.2
  5.4 0.6 copy-done.3
  6.0 15.0 %start.1.leaves = f32[1832,256]{1,0:T(8,128)} custom-call(s32[1]{0:T(128)} %bitcast.place_ref, f32[2,128]{1,0:T(2,128)} %copy-done.2, f32[2,128]{1,0:T(2,128)} %copy-done.3, f32[256,256]{1,0:T(8,128)} %f_hbm.1, f32[128,256]{1,0:T(8,128)} %h_hbm.1, f32[256,256]{1,0:T(8,128)} %q_hbm.1, f32[1,256]{1,0:T(1,128)} %bitcast.4, f32[256,256]{1,0:T(8,128)} %p_hbm.1), custom_call_target="tpu_custom_call" | custom-call | flops 2013265920 | bytes 920580 | tf_op jit(solution)/shard_map/start/pallas_call | solution.py:564
  21.0 0.0 copy-start
  21.0 1.5 copy-done
  22.5 2.6 %pair.1 = (f32[264,256]{1,0:T(8,128)S(1)}, f32[264,256]{1,0:T(8,128)S(1)}, f32[264,256]{1,0:T(8,128)S(1)}, f32[256,256]{1,0:T(8,128)S(1)}, f32[136,256]{1,0:T(8,128)S(1)}) custom-call(f32[1832,256]{1,0:T(8,128)S(1)} %copy-done), custom_call_target="tpu_custom_call" | custom-call | flops 671088640 | bytes 1875968 | tf_op jit(solution)/shard_map/pair/pallas_call | solution.py:564
  25.1 2.0 %resolve.9.solved = f32[264,256]{1,0:T(8,128)S(1)} custom-call(f32[264,256]{1,0:T(8,128)S(1)} %get-tuple-element.45.x_ref, f32[264,256]{1,0:T(8,128)S(1)} %get-tuple-element.46.y_ref), custom_call_target="tpu_custom_call" | custom-call | flops 2013265920 | bytes 540672 | tf_op jit(solution)/shard_map/resolve/pallas_call | solution.py:564
  27.2 10.8 %exchange_2.1 = (f32[264,256]{1,0:T(8,128)S(1)}, f32[264,256]{1,0:T(8,128)S(1)}, f32[264,256]{1,0:T(8,128)S(1)}, f32[256,256]{1,0:T(8,128)S(1)}, f32[136,256]{1,0:T(8,128)S(1)}) custom-call(f32[264,256]{1,0:T(8,128)S(1)} %resolve.9.solved, f32[264,256]{1,0:T(8,128)S(1)} %get-tuple-element.45.x_ref, f32[264,256]{1,0:T(8,128)S(1)} %get-tuple-element.46.y_ref, ...), custom_call_target="tpu_custom_call" | custom-call | flops 2013265920 | bytes 1482752 | tf_op jit(solution)/shard_map/exchange_2/pallas_call | solution.py:564
  38.0 2.3 %resolve.10.solved = f32[264,256]{1,0:T(8,128)S(1)} custom-call(f32[264,256]{1,0:T(8,128)S(1)} %get-tuple-element.50.x_ref, f32[264,256]{1,0:T(8,128)S(1)} %get-tuple-element.51.y_ref), custom_call_target="tpu_custom_call" | custom-call | flops 2013265920 | bytes 540672 | tf_op jit(solution)/shard_map/resolve/pallas_call | solution.py:564
  40.3 13.4 %exchange_4.1 = (f32[264,256]{1,0:T(8,128)S(1)}, f32[264,256]{1,0:T(8,128)S(1)}, f32[264,256]{1,0:T(8,128)S(1)}, f32[256,256]{1,0:T(8,128)S(1)}, f32[136,256]{1,0:T(8,128)S(1)}) custom-call(f32[264,256]{1,0:T(8,128)S(1)} %resolve.10.solved, f32[264,256]{1,0:T(8,128)S(1)} %get-tuple-element.50.x_ref, f32[264,256]{1,0:T(8,128)S(1)} %get-tuple-element.51.y_ref, ...), custom_call_target="tpu_custom_call" | custom-call | flops 2013265920 | bytes 1482752 | tf_op jit(solution)/shard_map/exchange_4/pallas_call | solution.py:564
  53.7 2.6 %resolve.11.solved = f32[264,256]{1,0:T(8,128)S(1)} custom-call(f32[264,256]{1,0:T(8,128)S(1)} %get-tuple-element.55.x_ref, f32[264,256]{1,0:T(8,128)S(1)} %get-tuple-element.56.y_ref), custom_call_target="tpu_custom_call" | custom-call | flops 2013265920 | bytes 540672 | tf_op jit(solution)/shard_map/resolve/pallas_call | solution.py:564
  56.3 10.9 %exchange_8.1 = (f32[264,256]{1,0:T(8,128)S(1)}, f32[264,256]{1,0:T(8,128)S(1)}, f32[264,256]{1,0:T(8,128)S(1)}, f32[256,256]{1,0:T(8,128)S(1)}, f32[136,256]{1,0:T(8,128)S(1)}) custom-call(f32[264,256]{1,0:T(8,128)S(1)} %resolve.11.solved, f32[264,256]{1,0:T(8,128)S(1)} %get-tuple-element.55.x_ref, f32[264,256]{1,0:T(8,128)S(1)} %get-tuple-element.56.y_ref, ...), custom_call_target="tpu_custom_call" | custom-call | flops 2013265920 | bytes 1482752 | tf_op jit(solution)/shard_map/exchange_8/pallas_call | solution.py:564
  67.1 2.6 %resolve.12.solved = f32[264,256]{1,0:T(8,128)S(1)} custom-call(f32[264,256]{1,0:T(8,128)S(1)} %get-tuple-element.60.x_ref, f32[264,256]{1,0:T(8,128)S(1)} %get-tuple-element.61.y_ref), custom_call_target="tpu_custom_call" | custom-call | flops 2013265920 | bytes 540672 | tf_op jit(solution)/shard_map/resolve/pallas_call | solution.py:564
  69.7 22.6 %exchange_16.1 = (f32[264,256]{1,0:T(8,128)S(1)}, f32[264,256]{1,0:T(8,128)S(1)}, f32[264,256]{1,0:T(8,128)S(1)}, f32[256,256]{1,0:T(8,128)S(1)}, f32[136,256]{1,0:T(8,128)S(1)}) custom-call(f32[264,256]{1,0:T(8,128)S(1)} %resolve.12.solved, f32[264,256]{1,0:T(8,128)S(1)} %get-tuple-element.60.x_ref, f32[264,256]{1,0:T(8,128)S(1)} %get-tuple-element.61.y_ref, ...), custom_call_target="tpu_custom_call" | custom-call | flops 2013265920 | bytes 1482752 | tf_op jit(solution)/shard_map/exchange_16/pallas_call | solution.py:564
  92.3 2.8 %resolve.13.solved = f32[264,256]{1,0:T(8,128)S(1)} custom-call(f32[264,256]{1,0:T(8,128)S(1)} %get-tuple-element.65.x_ref, f32[264,256]{1,0:T(8,128)S(1)} %get-tuple-element.66.y_ref), custom_call_target="tpu_custom_call" | custom-call | flops 2013265920 | bytes 540672 | tf_op jit(solution)/shard_map/resolve/pallas_call | solution.py:564
  95.1 24.0 %exchange_32.1 = (f32[264,256]{1,0:T(8,128)S(1)}, f32[264,256]{1,0:T(8,128)S(1)}, f32[264,256]{1,0:T(8,128)S(1)}, f32[256,256]{1,0:T(8,128)S(1)}, f32[136,256]{1,0:T(8,128)S(1)}) custom-call(f32[264,256]{1,0:T(8,128)S(1)} %resolve.13.solved, f32[264,256]{1,0:T(8,128)S(1)} %get-tuple-element.65.x_ref, f32[264,256]{1,0:T(8,128)S(1)} %get-tuple-element.66.y_ref, ...), custom_call_target="tpu_custom_call" | custom-call | flops 2013265920 | bytes 1482752 | tf_op jit(solution)/shard_map/exchange_32/pallas_call | solution.py:564
  119.2 3.1 %resolve.14.solved = f32[264,256]{1,0:T(8,128)S(1)} custom-call(f32[264,256]{1,0:T(8,128)S(1)} %get-tuple-element.70.x_ref, f32[264,256]{1,0:T(8,128)S(1)} %get-tuple-element.71.y_ref), custom_call_target="tpu_custom_call" | custom-call | flops 2013265920 | bytes 540672 | tf_op jit(solution)/shard_map/resolve/pallas_call | solution.py:564
  122.3 13.9 %exchange_64.1 = (f32[264,256]{1,0:T(8,128)S(1)}, f32[264,256]{1,0:T(8,128)S(1)}, f32[264,256]{1,0:T(8,128)S(1)}, f32[256,256]{1,0:T(8,128)S(1)}, f32[136,256]{1,0:T(8,128)S(1)}) custom-call(f32[264,256]{1,0:T(8,128)S(1)} %resolve.14.solved, f32[264,256]{1,0:T(8,128)S(1)} %get-tuple-element.70.x_ref, f32[264,256]{1,0:T(8,128)S(1)} %get-tuple-element.71.y_ref, ...), custom_call_target="tpu_custom_call" | custom-call | flops 2013265920 | bytes 1482752 | tf_op jit(solution)/shard_map/exchange_64/pallas_call | solution.py:564
  136.2 2.8 %resolve.15.solved = f32[264,256]{1,0:T(8,128)S(1)} custom-call(f32[264,256]{1,0:T(8,128)S(1)} %get-tuple-element.75.x_ref, f32[264,256]{1,0:T(8,128)S(1)} %get-tuple-element.76.y_ref), custom_call_target="tpu_custom_call" | custom-call | flops 2013265920 | bytes 540672 | tf_op jit(solution)/shard_map/resolve/pallas_call | solution.py:564
  139.0 0.0 copy-start.1
  139.0 12.4 %exchange_128.1 = (f32[264,256]{1,0:T(8,128)S(1)}, f32[264,256]{1,0:T(8,128)S(1)}, f32[264,256]{1,0:T(8,128)}, f32[8,256]{1,0:T(8,128)}, f32[8,256]{1,0:T(8,128)}) custom-call(f32[264,256]{1,0:T(8,128)S(1)} %resolve.15.solved, f32[264,256]{1,0:T(8,128)S(1)} %get-tuple-element.75.x_ref, f32[264,256]{1,0:T(8,128)S(1)} %get-tuple-element.76.y_ref, ...), custom_call_target="tpu_custom_call" | custom-call | flops 2013265920 | bytes 1482752 | tf_op jit(solution)/shard_map/exchange_128/pallas_call | solution.py:564
  151.4 0.0 copy-done.1
  151.5 2.3 %resolve.16.solved = f32[264,256]{1,0:T(8,128)S(1)} custom-call(f32[264,256]{1,0:T(8,128)S(1)} %get-tuple-element.82.x_ref, f32[264,256]{1,0:T(8,128)S(1)} %get-tuple-element.83.y_ref), custom_call_target="tpu_custom_call" | custom-call | flops 2013265920 | bytes 540672 | tf_op jit(solution)/shard_map/resolve/pallas_call | solution.py:564
  153.8 2.1 %finish.1 = (f32[264,256]{1,0:T(8,128)S(1)}, f32[264,256]{1,0:T(8,128)S(1)}) custom-call(f32[264,256]{1,0:T(8,128)S(1)} %resolve.16.solved, f32[264,256]{1,0:T(8,128)S(1)} %get-tuple-element.80.x_ref, f32[264,256]{1,0:T(8,128)S(1)} %get-tuple-element.81.y_ref, f32[1832,256]{1,0:T(8,128)S(1)} %copy-done.1), custom_call_target="tpu_custom_call" | custom-call | flops 2013265920 | bytes 2686976 | tf_op jit(solution)/shard_map/finish/pallas_call | solution.py:564
  155.9 2.9 %resolve.17.solved = f32[264,256]{1,0:T(8,128)S(1)} custom-call(f32[264,256]{1,0:T(8,128)S(1)} %get-tuple-element.84.x_ref.own_ref, f32[264,256]{1,0:T(8,128)S(1)} %get-tuple-element.85.y_ref.later_ref), custom_call_target="tpu_custom_call" | custom-call | flops 2013265920 | bytes 540672 | tf_op jit(solution)/shard_map/resolve/pallas_call | solution.py:564
  158.8 1.5 last.1
  (1 shorter events, 0.0 us)
Async XLA Ops:
  1.3 4.1 %copy-start.2 = (f32[2,128]{1,0:T(2,128)}, f32[2,128]{1,0:T(2,128)S(1)}, u32[]{:S(2)}) copy-start(f32[2,128]{1,0:T(2,128)S(1)} %pad_maximum_fusion.mine_ref) | copy-start | bytes 3076
  1.3 4.1 %collective-permute-start = (f32[2,128]{1,0:T(2,128)S(1)}, f32[2,128]{1,0:T(2,128)S(1)}, u32[]{:S(2)}, u32[]{:S(2)}) collective-permute-start(f32[2,128]{1,0:T(2,128)S(1)} %pad_maximum_fusion.mine_ref), channel_id=1, source_target_pairs={{0,1},{1,0},{2,3},{3,2},{4,5},{5,4},{6,7},{7,6},{8,9},{9,8},{10,11... | collective-permute-start | bytes 3080 | tf_op jit(solution)/shard_map/ppermute | solution.py:593
  5.4 0.6 copy-start.3
  21.0 1.5 copy-start
  139.0 12.4 %copy-start.1 = (f32[1832,256]{1,0:T(8,128)S(1)}, f32[1832,256]{1,0:T(8,128)}, u32[]{:S(2)}) copy-start(f32[1832,256]{1,0:T(8,128)} %start.1.leaves) | copy-start | bytes 5627908

commit v3 on v2

--- a/solution.py
+++ b/solution.py
@@ -224,12 +224,12 @@
         inner = inner_plain[...] * weights * weight
         active = jnp.where(first, 0.0, 1.0)
         mixed = inverse(inner, spectral_bound(inner, inner), half_pair)
-        gained = exact(mixed, gain)
+        gained = medium(mixed, gain)
         joined = exact(mixed, sensed)
         gain_t = gain.T
         error = y - exact(center[...], h_ref[...], NT) * weight
         leaves[pl.ds(at, ns), :] = active * (f_ref[...] - exact(gain_t, joined))
-        leaves[pl.ds(at + ns, ns), :] = noise[...] - exact(gain_t, gained)
+        leaves[pl.ds(at + ns, ns), :] = noise[...] - medium(gain_t, gained)
         leaves[pl.ds(at + 2 * ns, 8), :] = center[...] + exact(error, gained)
         leaves[pl.ds(at + ns + tall, ns), :] = active * medium(sensed.T, joined)
         leaves[pl.ds(at + 2 * ns + tall, 8), :] = active * exact(y, joined)
@@ -368,7 +368,7 @@
     spread_up = carry(spread_msg, spread_land, 2, 2, spread_hop)
     spread_side = carry(spread_msg, spread_land, 3, 2, 1)
     bind_down = carry(bind_msg, bind_land, 4, 3, -hop)
-    move_sends = jnp.logical_and(lead, reaches(hop))
+    move_sends = jnp.logical_and(jnp.logical_and(lead, reaches(hop)), mine >= hop)
     spread_sends = jnp.logical_and(lead, reaches(spread_hop))
     bind_sends = jnp.logical_and(side, reaches(-hop))
     spread_takes = jnp.logical_or(side, reaches(-spread_hop))
@@ -377,7 +377,7 @@
     else:
         move_up = carry(move_ref, move_land, 5, 0, hop)
         pull_up = carry(bind_ref, pull_land, 6, 1, hop)
-        move_takes = jnp.logical_or(side, reaches(-hop))
+        move_takes = jnp.logical_or(side, mine >= 2 * hop)
 
     pl.when(lead)(arrive)
     if not last:

time: 160 us -> 159 us (level)
  Pallas kernels: 153 us -> 151 us
where the time goes in v3:
time: 159 us
  Pallas kernels  151 us (95%)
  starting transfers between devices  3.28 us (2%)
  local copies, waits for them, and re-layouts  2.07 us (1%)
    pallas_call x21, Pallas kernels, call(): pl.pallas_call(kernel, out_shape=tuple((jax.ShapeDtypeStruct((r, width),...  151 us
    ppermute x1, starting transfers between devices, shards(): other = lax.ppermute(mine, 'tm', [(i, i ^ 1) for i in range(count)])  3.28 us
  transfers between devices with their start and end apart: 1, of which 1 were waited for; matrix products, arithmetic and copies ran while one was open for 0% of the time, Pallas kernels for 0%

profile of v3, /device:TPU:1, one launch (start us, length us, event | category | flops | bytes accessed | tf_op | source)
XLA Modules:
  0.0 159.0 jit_solution(12212249123673335687)
XLA Ops:
  0.6 0.7 pad_maximum_fusion.mine_ref
  1.3 0.0 copy-start.2
  1.3 3.3 %collective-permute-start = (f32[2,128]{1,0:T(2,128)S(1)}, f32[2,128]{1,0:T(2,128)S(1)}, u32[]{:S(2)}, u32[]{:S(2)}) collective-permute-start(f32[2,128]{1,0:T(2,128)S(1)} %pad_maximum_fusion.mine_ref), channel_id=1, source_target_pairs={{0,1},{1,0},{2,3},{3,2},{4,5},{5,4},{6,7},{7,6},{8,9},{9,8},{10,11... | collective-permute-start | bytes 3080 | tf_op jit(solution)/shard_map/ppermute | solution.py:593
  4.6 0.8 collective-permute-done.other_ref
  5.4 0.0 copy-start.3
  5.4 0.0 copy-done.2
  5.4 0.6 copy-done.3
  6.0 14.4 %start.1.leaves = f32[1832,256]{1,0:T(8,128)} custom-call(s32[1]{0:T(128)} %bitcast.place_ref, f32[2,128]{1,0:T(2,128)} %copy-done.2, f32[2,128]{1,0:T(2,128)} %copy-done.3, f32[256,256]{1,0:T(8,128)} %f_hbm.1, f32[128,256]{1,0:T(8,128)} %h_hbm.1, f32[256,256]{1,0:T(8,128)} %q_hbm.1, f32[1,256]{1,0:T(1,128)} %bitcast.4, f32[256,256]{1,0:T(8,128)} %p_hbm.1), custom_call_target="tpu_custom_call" | custom-call | flops 2013265920 | bytes 920580 | tf_op jit(solution)/shard_map/start/pallas_call | solution.py:564
  20.4 0.0 copy-start
  20.4 1.5 copy-done
  21.9 2.6 %pair.1 = (f32[264,256]{1,0:T(8,128)S(1)}, f32[264,256]{1,0:T(8,128)S(1)}, f32[264,256]{1,0:T(8,128)S(1)}, f32[256,256]{1,0:T(8,128)S(1)}, f32[136,256]{1,0:T(8,128)S(1)}) custom-call(f32[1832,256]{1,0:T(8,128)S(1)} %copy-done), custom_call_target="tpu_custom_call" | custom-call | flops 671088640 | bytes 1875968 | tf_op jit(solution)/shard_map/pair/pallas_call | solution.py:564
  24.6 2.0 %resolve.9.solved = f32[264,256]{1,0:T(8,128)S(1)} custom-call(f32[264,256]{1,0:T(8,128)S(1)} %get-tuple-element.45.x_ref, f32[264,256]{1,0:T(8,128)S(1)} %get-tuple-element.46.y_ref), custom_call_target="tpu_custom_call" | custom-call | flops 2013265920 | bytes 540672 | tf_op jit(solution)/shard_map/resolve/pallas_call | solution.py:564
  26.6 10.5 %exchange_2.1 = (f32[264,256]{1,0:T(8,128)S(1)}, f32[264,256]{1,0:T(8,128)S(1)}, f32[264,256]{1,0:T(8,128)S(1)}, f32[256,256]{1,0:T(8,128)S(1)}, f32[136,256]{1,0:T(8,128)S(1)}) custom-call(f32[264,256]{1,0:T(8,128)S(1)} %resolve.9.solved, f32[264,256]{1,0:T(8,128)S(1)} %get-tuple-element.45.x_ref, f32[264,256]{1,0:T(8,128)S(1)} %get-tuple-element.46.y_ref, ...), custom_call_target="tpu_custom_call" | custom-call | flops 2013265920 | bytes 1482752 | tf_op jit(solution)/shard_map/exchange_2/pallas_call | solution.py:564
  37.1 2.3 %resolve.10.solved = f32[264,256]{1,0:T(8,128)S(1)} custom-call(f32[264,256]{1,0:T(8,128)S(1)} %get-tuple-element.50.x_ref, f32[264,256]{1,0:T(8,128)S(1)} %get-tuple-element.51.y_ref), custom_call_target="tpu_custom_call" | custom-call | flops 2013265920 | bytes 540672 | tf_op jit(solution)/shard_map/resolve/pallas_call | solution.py:564
  39.5 13.7 %exchange_4.1 = (f32[264,256]{1,0:T(8,128)S(1)}, f32[264,256]{1,0:T(8,128)S(1)}, f32[264,256]{1,0:T(8,128)S(1)}, f32[256,256]{1,0:T(8,128)S(1)}, f32[136,256]{1,0:T(8,128)S(1)}) custom-call(f32[264,256]{1,0:T(8,128)S(1)} %resolve.10.solved, f32[264,256]{1,0:T(8,128)S(1)} %get-tuple-element.50.x_ref, f32[264,256]{1,0:T(8,128)S(1)} %get-tuple-element.51.y_ref, ...), custom_call_target="tpu_custom_call" | custom-call | flops 2013265920 | bytes 1482752 | tf_op jit(solution)/shard_map/exchange_4/pallas_call | solution.py:564
  53.1 2.6 %resolve.11.solved = f32[264,256]{1,0:T(8,128)S(1)} custom-call(f32[264,256]{1,0:T(8,128)S(1)} %get-tuple-element.55.x_ref, f32[264,256]{1,0:T(8,128)S(1)} %get-tuple-element.56.y_ref), custom_call_target="tpu_custom_call" | custom-call | flops 2013265920 | bytes 540672 | tf_op jit(solution)/shard_map/resolve/pallas_call | solution.py:564
  55.7 10.5 %exchange_8.1 = (f32[264,256]{1,0:T(8,128)S(1)}, f32[264,256]{1,0:T(8,128)S(1)}, f32[264,256]{1,0:T(8,128)S(1)}, f32[256,256]{1,0:T(8,128)S(1)}, f32[136,256]{1,0:T(8,128)S(1)}) custom-call(f32[264,256]{1,0:T(8,128)S(1)} %resolve.11.solved, f32[264,256]{1,0:T(8,128)S(1)} %get-tuple-element.55.x_ref, f32[264,256]{1,0:T(8,128)S(1)} %get-tuple-element.56.y_ref, ...), custom_call_target="tpu_custom_call" | custom-call | flops 2013265920 | bytes 1482752 | tf_op jit(solution)/shard_map/exchange_8/pallas_call | solution.py:564
  66.2 2.6 %resolve.12.solved = f32[264,256]{1,0:T(8,128)S(1)} custom-call(f32[264,256]{1,0:T(8,128)S(1)} %get-tuple-element.60.x_ref, f32[264,256]{1,0:T(8,128)S(1)} %get-tuple-element.61.y_ref), custom_call_target="tpu_custom_call" | custom-call | flops 2013265920 | bytes 540672 | tf_op jit(solution)/shard_map/resolve/pallas_call | solution.py:564
  68.8 23.0 %exchange_16.1 = (f32[264,256]{1,0:T(8,128)S(1)}, f32[264,256]{1,0:T(8,128)S(1)}, f32[264,256]{1,0:T(8,128)S(1)}, f32[256,256]{1,0:T(8,128)S(1)}, f32[136,256]{1,0:T(8,128)S(1)}) custom-call(f32[264,256]{1,0:T(8,128)S(1)} %resolve.12.solved, f32[264,256]{1,0:T(8,128)S(1)} %get-tuple-element.60.x_ref, f32[264,256]{1,0:T(8,128)S(1)} %get-tuple-element.61.y_ref, ...), custom_call_target="tpu_custom_call" | custom-call | flops 2013265920 | bytes 1482752 | tf_op jit(solution)/shard_map/exchange_16/pallas_call | solution.py:564
  91.8 2.8 %resolve.13.solved = f32[264,256]{1,0:T(8,128)S(1)} custom-call(f32[264,256]{1,0:T(8,128)S(1)} %get-tuple-element.65.x_ref, f32[264,256]{1,0:T(8,128)S(1)} %get-tuple-element.66.y_ref), custom_call_target="tpu_custom_call" | custom-call | flops 2013265920 | bytes 540672 | tf_op jit(solution)/shard_map/resolve/pallas_call | solution.py:564
  94.6 22.8 %exchange_32.1 = (f32[264,256]{1,0:T(8,128)S(1)}, f32[264,256]{1,0:T(8,128)S(1)}, f32[264,256]{1,0:T(8,128)S(1)}, f32[256,256]{1,0:T(8,128)S(1)}, f32[136,256]{1,0:T(8,128)S(1)}) custom-call(f32[264,256]{1,0:T(8,128)S(1)} %resolve.13.solved, f32[264,256]{1,0:T(8,128)S(1)} %get-tuple-element.65.x_ref, f32[264,256]{1,0:T(8,128)S(1)} %get-tuple-element.66.y_ref, ...), custom_call_target="tpu_custom_call" | custom-call | flops 2013265920 | bytes 1482752 | tf_op jit(solution)/shard_map/exchange_32/pallas_call | solution.py:564
  117.5 2.8 %resolve.14.solved = f32[264,256]{1,0:T(8,128)S(1)} custom-call(f32[264,256]{1,0:T(8,128)S(1)} %get-tuple-element.70.x_ref, f32[264,256]{1,0:T(8,128)S(1)} %get-tuple-element.71.y_ref), custom_call_target="tpu_custom_call" | custom-call | flops 2013265920 | bytes 540672 | tf_op jit(solution)/shard_map/resolve/pallas_call | solution.py:564
  120.3 15.3 %exchange_64.1 = (f32[264,256]{1,0:T(8,128)S(1)}, f32[264,256]{1,0:T(8,128)S(1)}, f32[264,256]{1,0:T(8,128)S(1)}, f32[256,256]{1,0:T(8,128)S(1)}, f32[136,256]{1,0:T(8,128)S(1)}) custom-call(f32[264,256]{1,0:T(8,128)S(1)} %resolve.14.solved, f32[264,256]{1,0:T(8,128)S(1)} %get-tuple-element.70.x_ref, f32[264,256]{1,0:T(8,128)S(1)} %get-tuple-element.71.y_ref, ...), custom_call_target="tpu_custom_call" | custom-call | flops 2013265920 | bytes 1482752 | tf_op jit(solution)/shard_map/exchange_64/pallas_call | solution.py:564
  135.7 2.9 %resolve.15.solved = f32[264,256]{1,0:T(8,128)S(1)} custom-call(f32[264,256]{1,0:T(8,128)S(1)} %get-tuple-element.75.x_ref, f32[264,256]{1,0:T(8,128)S(1)} %get-tuple-element.76.y_ref), custom_call_target="tpu_custom_call" | custom-call | flops 2013265920 | bytes 540672 | tf_op jit(solution)/shard_map/resolve/pallas_call | solution.py:564
  138.5 0.0 copy-start.1
  138.6 11.6 %exchange_128.1 = (f32[264,256]{1,0:T(8,128)S(1)}, f32[264,256]{1,0:T(8,128)S(1)}, f32[264,256]{1,0:T(8,128)}, f32[8,256]{1,0:T(8,128)}, f32[8,256]{1,0:T(8,128)}) custom-call(f32[264,256]{1,0:T(8,128)S(1)} %resolve.15.solved, f32[264,256]{1,0:T(8,128)S(1)} %get-tuple-element.75.x_ref, f32[264,256]{1,0:T(8,128)S(1)} %get-tuple-element.76.y_ref, ...), custom_call_target="tpu_custom_call" | custom-call | flops 2013265920 | bytes 1482752 | tf_op jit(solution)/shard_map/exchange_128/pallas_call | solution.py:564
  150.2 0.0 copy-done.1
  150.2 2.3 %resolve.16.solved = f32[264,256]{1,0:T(8,128)S(1)} custom-call(f32[264,256]{1,0:T(8,128)S(1)} %get-tuple-element.82.x_ref, f32[264,256]{1,0:T(8,128)S(1)} %get-tuple-element.83.y_ref), custom_call_target="tpu_custom_call" | custom-call | flops 2013265920 | bytes 540672 | tf_op jit(solution)/shard_map/resolve/pallas_call | solution.py:564
  152.5 2.1 %finish.1 = (f32[264,256]{1,0:T(8,128)S(1)}, f32[264,256]{1,0:T(8,128)S(1)}) custom-call(f32[264,256]{1,0:T(8,128)S(1)} %resolve.16.solved, f32[264,256]{1,0:T(8,128)S(1)} %get-tuple-element.80.x_ref, f32[264,256]{1,0:T(8,128)S(1)} %get-tuple-element.81.y_ref, f32[1832,256]{1,0:T(8,128)S(1)} %copy-done.1), custom_call_target="tpu_custom_call" | custom-call | flops 2013265920 | bytes 2686976 | tf_op jit(solution)/shard_map/finish/pallas_call | solution.py:564
  154.6 2.9 %resolve.17.solved = f32[264,256]{1,0:T(8,128)S(1)} custom-call(f32[264,256]{1,0:T(8,128)S(1)} %get-tuple-element.84.x_ref.own_ref, f32[264,256]{1,0:T(8,128)S(1)} %get-tuple-element.85.y_ref.later_ref), custom_call_target="tpu_custom_call" | custom-call | flops 2013265920 | bytes 540672 | tf_op jit(solution)/shard_map/resolve/pallas_call | solution.py:564
  157.5 1.5 last.1
  (1 shorter events, 0.0 us)
Async XLA Ops:
  1.3 4.1 %copy-start.2 = (f32[2,128]{1,0:T(2,128)}, f32[2,128]{1,0:T(2,128)S(1)}, u32[]{:S(2)}) copy-start(f32[2,128]{1,0:T(2,128)S(1)} %pad_maximum_fusion.mine_ref) | copy-start | bytes 3076
  1.3 4.1 %collective-permute-start = (f32[2,128]{1,0:T(2,128)S(1)}, f32[2,128]{1,0:T(2,128)S(1)}, u32[]{:S(2)}, u32[]{:S(2)}) collective-permute-start(f32[2,128]{1,0:T(2,128)S(1)} %pad_maximum_fusion.mine_ref), channel_id=1, source_target_pairs={{0,1},{1,0},{2,3},{3,2},{4,5},{5,4},{6,7},{7,6},{8,9},{9,8},{10,11... | collective-permute-start | bytes 3080 | tf_op jit(solution)/shard_map/ppermute | solution.py:593
  5.4 0.6 copy-start.3
  20.4 1.5 copy-start
  138.5 11.6 %copy-start.1 = (f32[1832,256]{1,0:T(8,128)S(1)}, f32[1832,256]{1,0:T(8,128)}, u32[]{:S(2)}) copy-start(f32[1832,256]{1,0:T(8,128)} %start.1.leaves) | copy-start | bytes 5627908

commit v4 on v3

--- a/solution.py
+++ b/solution.py
@@ -190,6 +190,8 @@
     ]
     for copy in copies:
         copy.start()
+    prior_copy = pltpu.make_async_copy(p_hbm, p_ref, sems.at[3])
+    pl.when(chip == 0)(prior_copy.start)
     center[...] = jnp.zeros_like(center)
     eye = unit(no)
     copies[0].wait()
@@ -204,9 +206,7 @@
 
         @pl.when(first)
         def _():
-            copy = pltpu.make_async_copy(p_hbm, p_ref, sems.at[3])
-            copy.start()
-            copy.wait()
+            prior_copy.wait()
             noise[...] += exact(exact(f_ref[...], p_ref[...]), f_ref[...], NT)
             center[...] = exact(jnp.broadcast_to(m_ref[...], center.shape), f_ref[...], NT)
 

time: 159 us -> 159 us (level)
  no operation moved by 1% of the time
where the time goes in v4:
time: 159 us
  Pallas kernels  151 us (95%)
  starting transfers between devices  3.28 us (2%)
  local copies, waits for them, and re-layouts  2.07 us (1%)
    pallas_call x21, Pallas kernels, call(): pl.pallas_call(kernel, out_shape=tuple((jax.ShapeDtypeStruct((r, width),...  151 us
    ppermute x1, starting transfers between devices, shards(): other = lax.ppermute(mine, 'tm', [(i, i ^ 1) for i in range(count)])  3.28 us
  transfers between devices with their start and end apart: 1, of which 1 were waited for; matrix products, arithmetic and copies ran while one was open for 0% of the time, Pallas kernels for 0%

profile of v4, /device:TPU:1, one launch (start us, length us, event | category | flops | bytes accessed | tf_op | source)
XLA Modules:
  0.0 158.8 jit_solution(10233924782859235722)
XLA Ops:
  0.6 0.7 pad_maximum_fusion.mine_ref
  1.3 0.0 copy-start.2
  1.3 3.3 %collective-permute-start = (f32[2,128]{1,0:T(2,128)S(1)}, f32[2,128]{1,0:T(2,128)S(1)}, u32[]{:S(2)}, u32[]{:S(2)}) collective-permute-start(f32[2,128]{1,0:T(2,128)S(1)} %pad_maximum_fusion.mine_ref), channel_id=1, source_target_pairs={{0,1},{1,0},{2,3},{3,2},{4,5},{5,4},{6,7},{7,6},{8,9},{9,8},{10,11... | collective-permute-start | bytes 3080 | tf_op jit(solution)/shard_map/ppermute | solution.py:593
  4.6 0.8 collective-permute-done.other_ref
  5.4 0.0 copy-start.3
  5.4 0.0 copy-done.2
  5.4 0.6 copy-done.3
  6.0 13.5 %start.1.leaves = f32[1832,256]{1,0:T(8,128)} custom-call(s32[1]{0:T(128)} %bitcast.place_ref, f32[2,128]{1,0:T(2,128)} %copy-done.2, f32[2,128]{1,0:T(2,128)} %copy-done.3, f32[256,256]{1,0:T(8,128)} %f_hbm.1, f32[128,256]{1,0:T(8,128)} %h_hbm.1, f32[256,256]{1,0:T(8,128)} %q_hbm.1, f32[1,256]{1,0:T(1,128)} %bitcast.4, f32[256,256]{1,0:T(8,128)} %p_hbm.1), custom_call_target="tpu_custom_call" | custom-call | flops 2013265920 | bytes 920580 | tf_op jit(solution)/shard_map/start/pallas_call | solution.py:564
  19.5 0.0 copy-start
  19.5 1.5 copy-done
  21.0 2.6 %pair.1 = (f32[264,256]{1,0:T(8,128)S(1)}, f32[264,256]{1,0:T(8,128)S(1)}, f32[264,256]{1,0:T(8,128)S(1)}, f32[256,256]{1,0:T(8,128)S(1)}, f32[136,256]{1,0:T(8,128)S(1)}) custom-call(f32[1832,256]{1,0:T(8,128)S(1)} %copy-done), custom_call_target="tpu_custom_call" | custom-call | flops 671088640 | bytes 1875968 | tf_op jit(solution)/shard_map/pair/pallas_call | solution.py:564
  23.6 2.0 %resolve.9.solved = f32[264,256]{1,0:T(8,128)S(1)} custom-call(f32[264,256]{1,0:T(8,128)S(1)} %get-tuple-element.45.x_ref, f32[264,256]{1,0:T(8,128)S(1)} %get-tuple-element.46.y_ref), custom_call_target="tpu_custom_call" | custom-call | flops 2013265920 | bytes 540672 | tf_op jit(solution)/shard_map/resolve/pallas_call | solution.py:564
  25.6 10.8 %exchange_2.1 = (f32[264,256]{1,0:T(8,128)S(1)}, f32[264,256]{1,0:T(8,128)S(1)}, f32[264,256]{1,0:T(8,128)S(1)}, f32[256,256]{1,0:T(8,128)S(1)}, f32[136,256]{1,0:T(8,128)S(1)}) custom-call(f32[264,256]{1,0:T(8,128)S(1)} %resolve.9.solved, f32[264,256]{1,0:T(8,128)S(1)} %get-tuple-element.45.x_ref, f32[264,256]{1,0:T(8,128)S(1)} %get-tuple-element.46.y_ref, ...), custom_call_target="tpu_custom_call" | custom-call | flops 2013265920 | bytes 1482752 | tf_op jit(solution)/shard_map/exchange_2/pallas_call | solution.py:564
  36.5 2.3 %resolve.10.solved = f32[264,256]{1,0:T(8,128)S(1)} custom-call(f32[264,256]{1,0:T(8,128)S(1)} %get-tuple-element.50.x_ref, f32[264,256]{1,0:T(8,128)S(1)} %get-tuple-element.51.y_ref), custom_call_target="tpu_custom_call" | custom-call | flops 2013265920 | bytes 540672 | tf_op jit(solution)/shard_map/resolve/pallas_call | solution.py:564
  38.8 13.4 %exchange_4.1 = (f32[264,256]{1,0:T(8,128)S(1)}, f32[264,256]{1,0:T(8,128)S(1)}, f32[264,256]{1,0:T(8,128)S(1)}, f32[256,256]{1,0:T(8,128)S(1)}, f32[136,256]{1,0:T(8,128)S(1)}) custom-call(f32[264,256]{1,0:T(8,128)S(1)} %resolve.10.solved, f32[264,256]{1,0:T(8,128)S(1)} %get-tuple-element.50.x_ref, f32[264,256]{1,0:T(8,128)S(1)} %get-tuple-element.51.y_ref, ...), custom_call_target="tpu_custom_call" | custom-call | flops 2013265920 | bytes 1482752 | tf_op jit(solution)/shard_map/exchange_4/pallas_call | solution.py:564
  52.2 2.6 %resolve.11.solved = f32[264,256]{1,0:T(8,128)S(1)} custom-call(f32[264,256]{1,0:T(8,128)S(1)} %get-tuple-element.55.x_ref, f32[264,256]{1,0:T(8,128)S(1)} %get-tuple-element.56.y_ref), custom_call_target="tpu_custom_call" | custom-call | flops 2013265920 | bytes 540672 | tf_op jit(solution)/shard_map/resolve/pallas_call | solution.py:564
  54.8 11.7 %exchange_8.1 = (f32[264,256]{1,0:T(8,128)S(1)}, f32[264,256]{1,0:T(8,128)S(1)}, f32[264,256]{1,0:T(8,128)S(1)}, f32[256,256]{1,0:T(8,128)S(1)}, f32[136,256]{1,0:T(8,128)S(1)}) custom-call(f32[264,256]{1,0:T(8,128)S(1)} %resolve.11.solved, f32[264,256]{1,0:T(8,128)S(1)} %get-tuple-element.55.x_ref, f32[264,256]{1,0:T(8,128)S(1)} %get-tuple-element.56.y_ref, ...), custom_call_target="tpu_custom_call" | custom-call | flops 2013265920 | bytes 1482752 | tf_op jit(solution)/shard_map/exchange_8/pallas_call | solution.py:564
  66.5 2.6 %resolve.12.solved = f32[264,256]{1,0:T(8,128)S(1)} custom-call(f32[264,256]{1,0:T(8,128)S(1)} %get-tuple-element.60.x_ref, f32[264,256]{1,0:T(8,128)S(1)} %get-tuple-element.61.y_ref), custom_call_target="tpu_custom_call" | custom-call | flops 2013265920 | bytes 540672 | tf_op jit(solution)/shard_map/resolve/pallas_call | solution.py:564
  69.1 22.8 %exchange_16.1 = (f32[264,256]{1,0:T(8,128)S(1)}, f32[264,256]{1,0:T(8,128)S(1)}, f32[264,256]{1,0:T(8,128)S(1)}, f32[256,256]{1,0:T(8,128)S(1)}, f32[136,256]{1,0:T(8,128)S(1)}) custom-call(f32[264,256]{1,0:T(8,128)S(1)} %resolve.12.solved, f32[264,256]{1,0:T(8,128)S(1)} %get-tuple-element.60.x_ref, f32[264,256]{1,0:T(8,128)S(1)} %get-tuple-element.61.y_ref, ...), custom_call_target="tpu_custom_call" | custom-call | flops 2013265920 | bytes 1482752 | tf_op jit(solution)/shard_map/exchange_16/pallas_call | solution.py:564
  91.9 2.8 %resolve.13.solved = f32[264,256]{1,0:T(8,128)S(1)} custom-call(f32[264,256]{1,0:T(8,128)S(1)} %get-tuple-element.65.x_ref, f32[264,256]{1,0:T(8,128)S(1)} %get-tuple-element.66.y_ref), custom_call_target="tpu_custom_call" | custom-call | flops 2013265920 | bytes 540672 | tf_op jit(solution)/shard_map/resolve/pallas_call | solution.py:564
  94.8 22.8 %exchange_32.1 = (f32[264,256]{1,0:T(8,128)S(1)}, f32[264,256]{1,0:T(8,128)S(1)}, f32[264,256]{1,0:T(8,128)S(1)}, f32[256,256]{1,0:T(8,128)S(1)}, f32[136,256]{1,0:T(8,128)S(1)}) custom-call(f32[264,256]{1,0:T(8,128)S(1)} %resolve.13.solved, f32[264,256]{1,0:T(8,128)S(1)} %get-tuple-element.65.x_ref, f32[264,256]{1,0:T(8,128)S(1)} %get-tuple-element.66.y_ref, ...), custom_call_target="tpu_custom_call" | custom-call | flops 2013265920 | bytes 1482752 | tf_op jit(solution)/shard_map/exchange_32/pallas_call | solution.py:564
  117.6 2.8 %resolve.14.solved = f32[264,256]{1,0:T(8,128)S(1)} custom-call(f32[264,256]{1,0:T(8,128)S(1)} %get-tuple-element.70.x_ref, f32[264,256]{1,0:T(8,128)S(1)} %get-tuple-element.71.y_ref), custom_call_target="tpu_custom_call" | custom-call | flops 2013265920 | bytes 540672 | tf_op jit(solution)/shard_map/resolve/pallas_call | solution.py:564
  120.5 15.3 %exchange_64.1 = (f32[264,256]{1,0:T(8,128)S(1)}, f32[264,256]{1,0:T(8,128)S(1)}, f32[264,256]{1,0:T(8,128)S(1)}, f32[256,256]{1,0:T(8,128)S(1)}, f32[136,256]{1,0:T(8,128)S(1)}) custom-call(f32[264,256]{1,0:T(8,128)S(1)} %resolve.14.solved, f32[264,256]{1,0:T(8,128)S(1)} %get-tuple-element.70.x_ref, f32[264,256]{1,0:T(8,128)S(1)} %get-tuple-element.71.y_ref, ...), custom_call_target="tpu_custom_call" | custom-call | flops 2013265920 | bytes 1482752 | tf_op jit(solution)/shard_map/exchange_64/pallas_call | solution.py:564
  135.8 2.9 %resolve.15.solved = f32[264,256]{1,0:T(8,128)S(1)} custom-call(f32[264,256]{1,0:T(8,128)S(1)} %get-tuple-element.75.x_ref, f32[264,256]{1,0:T(8,128)S(1)} %get-tuple-element.76.y_ref), custom_call_target="tpu_custom_call" | custom-call | flops 2013265920 | bytes 540672 | tf_op jit(solution)/shard_map/resolve/pallas_call | solution.py:564
  138.7 0.0 copy-start.1
  138.7 11.2 %exchange_128.1 = (f32[264,256]{1,0:T(8,128)S(1)}, f32[264,256]{1,0:T(8,128)S(1)}, f32[264,256]{1,0:T(8,128)}, f32[8,256]{1,0:T(8,128)}, f32[8,256]{1,0:T(8,128)}) custom-call(f32[264,256]{1,0:T(8,128)S(1)} %resolve.15.solved, f32[264,256]{1,0:T(8,128)S(1)} %get-tuple-element.75.x_ref, f32[264,256]{1,0:T(8,128)S(1)} %get-tuple-element.76.y_ref, ...), custom_call_target="tpu_custom_call" | custom-call | flops 2013265920 | bytes 1482752 | tf_op jit(solution)/shard_map/exchange_128/pallas_call | solution.py:564
  149.9 0.0 copy-done.1
  150.0 2.3 %resolve.16.solved = f32[264,256]{1,0:T(8,128)S(1)} custom-call(f32[264,256]{1,0:T(8,128)S(1)} %get-tuple-element.82.x_ref, f32[264,256]{1,0:T(8,128)S(1)} %get-tuple-element.83.y_ref), custom_call_target="tpu_custom_call" | custom-call | flops 2013265920 | bytes 540672 | tf_op jit(solution)/shard_map/resolve/pallas_call | solution.py:564
  152.3 2.1 %finish.1 = (f32[264,256]{1,0:T(8,128)S(1)}, f32[264,256]{1,0:T(8,128)S(1)}) custom-call(f32[264,256]{1,0:T(8,128)S(1)} %resolve.16.solved, f32[264,256]{1,0:T(8,128)S(1)} %get-tuple-element.80.x_ref, f32[264,256]{1,0:T(8,128)S(1)} %get-tuple-element.81.y_ref, f32[1832,256]{1,0:T(8,128)S(1)} %copy-done.1), custom_call_target="tpu_custom_call" | custom-call | flops 2013265920 | bytes 2686976 | tf_op jit(solution)/shard_map/finish/pallas_call | solution.py:564
  154.4 2.9 %resolve.17.solved = f32[264,256]{1,0:T(8,128)S(1)} custom-call(f32[264,256]{1,0:T(8,128)S(1)} %get-tuple-element.84.x_ref.own_ref, f32[264,256]{1,0:T(8,128)S(1)} %get-tuple-element.85.y_ref.later_ref), custom_call_target="tpu_custom_call" | custom-call | flops 2013265920 | bytes 540672 | tf_op jit(solution)/shard_map/resolve/pallas_call | solution.py:564
  157.3 1.5 last.1
  (1 shorter events, 0.0 us)
Async XLA Ops:
  1.3 4.1 %copy-start.2 = (f32[2,128]{1,0:T(2,128)}, f32[2,128]{1,0:T(2,128)S(1)}, u32[]{:S(2)}) copy-start(f32[2,128]{1,0:T(2,128)S(1)} %pad_maximum_fusion.mine_ref) | copy-start | bytes 3076
  1.3 4.1 %collective-permute-start = (f32[2,128]{1,0:T(2,128)S(1)}, f32[2,128]{1,0:T(2,128)S(1)}, u32[]{:S(2)}, u32[]{:S(2)}) collective-permute-start(f32[2,128]{1,0:T(2,128)S(1)} %pad_maximum_fusion.mine_ref), channel_id=1, source_target_pairs={{0,1},{1,0},{2,3},{3,2},{4,5},{5,4},{6,7},{7,6},{8,9},{9,8},{10,11... | collective-permute-start | bytes 3080 | tf_op jit(solution)/shard_map/ppermute | solution.py:593
  5.4 0.6 copy-start.3
  19.5 1.5 copy-start
  138.7 11.3 %copy-start.1 = (f32[1832,256]{1,0:T(8,128)S(1)}, f32[1832,256]{1,0:T(8,128)}, u32[]{:S(2)}) copy-start(f32[1832,256]{1,0:T(8,128)} %start.1.leaves) | copy-start | bytes 5627908
